TPU v7x, 128 devices: a whole 4x4x4 slice. The times are simulated.
128 devices in a mesh: sn: 32 (over x, y, core), rhs: 4 (over z).
Axes of the slice: x: 4, y: 4, z: 4, core: 2. Of those that a mesh axis runs over, the one named last changes fastest.
Arguments:
- rhs_leaf: float32 [1024, 256, 128], P('sn', 'rhs'), may hold values from -6 to 6
- rhs_top: float32 [32, 256, 128], P('sn', 'rhs'), may hold values from -6 to 6
- leaf_blocks: float32 [1024, 3, 128, 128], P('sn', None, 'rhs'), may hold values from -0.078125 to 0.078125
- leaf_dinv: float32 [1024, 128, 128], P('sn', 'rhs')
- leaf_struct: int32 [1024, 3], P('sn'), may hold values from 1 to 63, as said below
- top_blocks: float32 [32, 32, 128, 128], P(None, 'sn', 'rhs'), may hold values from -0.1875 to 0.1875
- top_dinv: float32 [32, 128, 128], P('sn', 'rhs')
Outputs:
- leaf_solution: float32 [1024, 256, 128], P('sn', 'rhs')
- top_solution: float32 [32, 256, 128], P('sn', 'rhs')
Inputs may be any that keep to these rules, and one draw needn't show every extreme that they name: `leaf_struct`: subtree d hangs below top supernode a = 4 * (d // 4). Row d * 32 + s names 3 distinct ancestors of leaf supernode s of subtree d: a value v < 32 is supernode v of the same subtree, with v > s; a value 32 + k is a top supernode k on a's path to the root, that is k = a or the factor holds top block (k, a). Column 0 is the elimination tree parent: s + 1, except for the subtree's last supernode, whose parent is 32 + a.
All inputs are finite; a program needn't handle non-finite values.
Results may differ from a plain program's by a relative error of at most 0.00018.
Values sent between devices are 32-bit elements; how exact they have to be, the bound alone decides.
A program may use at most 64 MiB of HBM per device.

v0:
```python
import jax
import jax.numpy as jnp
from jax import lax
from jax.sharding import PartitionSpec as P

highest = lax.Precision.HIGHEST


def top_levels(count):
    levels = count.bit_length()
    index = jnp.arange(count, dtype=jnp.int32)
    depth_of = jnp.zeros((count,), jnp.int32)
    span = jnp.ones((count,), jnp.int32)
    for place in range(levels):
        hit = ((index + 1) % 2 ** (place + 1) == 0).astype(jnp.int32)
        depth_of = depth_of + hit
        span = span + hit * 2**place
    row_index = index[:, None]
    col_index = index[None, :]
    keep = (col_index < row_index) & (col_index >= row_index + 1 - span[:, None])
    return (depth_of, keep.astype(jnp.float32))


def leaf_forward(top_total, rhs_part, blocks, inverses, struct):
    leaf_total = rhs_part.shape[0]
    updates = jnp.zeros((leaf_total + top_total,) + rhs_part.shape[1:], jnp.float32)
    values = jnp.zeros(rhs_part.shape, jnp.float32)

    def advance(position, state_pair):
        updates, values = state_pair
        source = lax.dynamic_index_in_dim(rhs_part, position, 0, False) - lax.dynamic_index_in_dim(
            updates, position, 0, False
        )
        solved = jnp.einsum(
            "ck,ik->ci",
            source,
            lax.dynamic_index_in_dim(inverses, position, 0, False),
            precision=highest,
        )
        targets = lax.dynamic_index_in_dim(struct, position, 0, False)
        outgoing = jnp.einsum(
            "ck,rik->rci",
            solved,
            lax.dynamic_index_in_dim(blocks, position, 0, False),
            precision=highest,
        )
        updates = updates.at[targets].add(outgoing)
        values = lax.dynamic_update_index_in_dim(values, solved, position, 0)
        return (updates, values)

    updates, values = lax.fori_loop(0, leaf_total, advance, (updates, values))
    return (values, updates[leaf_total:])


def leaf_backward(forward_values, blocks, inverses, struct, top_values):
    leaf_total = forward_values.shape[0]
    solution_buffer = jnp.concatenate([jnp.zeros_like(forward_values), top_values], axis=0)

    def retreat(offset, solution_buffer):
        position = leaf_total - 1 - offset
        targets = lax.dynamic_index_in_dim(struct, position, 0, False)
        ancestors = jnp.take(solution_buffer, targets, axis=0)
        summed = jnp.einsum(
            "rci,rik->ck",
            ancestors,
            lax.dynamic_index_in_dim(blocks, position, 0, False),
            precision=highest,
        )
        own_rhs = lax.dynamic_index_in_dim(forward_values, position, 0, False)
        solved = jnp.einsum(
            "ci,ik->ck",
            own_rhs - summed,
            lax.dynamic_index_in_dim(inverses, position, 0, False),
            precision=highest,
        )
        return lax.dynamic_update_index_in_dim(solution_buffer, solved, position, 0)

    solution_buffer = lax.fori_loop(0, leaf_total, retreat, solution_buffer)
    return solution_buffer[:leaf_total]


def forward_by_rows(top_source, masked_rows, own_inverse, my_level, levels, pull_values):
    forward_own = jnp.zeros_like(top_source)
    for level in range(levels):
        if level == 0:
            pulled = jnp.zeros_like(top_source)
        else:
            gathered = pull_values(forward_own[None])
            pulled = jnp.einsum("jck,jik->ci", gathered, masked_rows, precision=highest)
        candidate = jnp.einsum("ck,ik->ci", top_source - pulled, own_inverse, precision=highest)
        forward_own = jnp.where(my_level == level, candidate, forward_own)
    return forward_own


def backward_by_rows(forward_own, masked_rows, own_inverse, my_level, levels, sum_terms):
    backward_own = jnp.zeros_like(forward_own)
    pushed = jnp.zeros_like(forward_own)
    for level in range(levels - 1, -1, -1):
        candidate = jnp.einsum("ci,ik->ck", forward_own - pushed, own_inverse, precision=highest)
        backward_own = jnp.where(my_level == level, candidate, backward_own)
        if level > 0:
            sender = (my_level == level).astype(jnp.float32)
            outgoing = (
                jnp.einsum("ci,tik->tck", backward_own, masked_rows, precision=highest) * sender
            )
            pushed = pushed + sum_terms(outgoing)[0]
    return backward_own


def local(rhs_leaf, rhs_top, leaf_blocks, leaf_dinv, leaf_struct, top_blocks, top_dinv):
    blocks, inverses, top_cols, top_inverse = (
        lax.all_gather(leaf_blocks, "rhs", axis=2, tiled=True),
        lax.all_gather(leaf_dinv, "rhs", axis=1, tiled=True),
        lax.all_gather(top_blocks, "rhs", axis=2, tiled=True),
        lax.all_gather(top_dinv, "rhs", axis=1, tiled=True),
    )
    top_total = top_cols.shape[0]
    levels = top_total.bit_length()
    my_index = lax.axis_index("sn")
    depth_of, keep = top_levels(top_total)
    my_level = lax.dynamic_index_in_dim(depth_of, my_index, 0, False)
    own_inverse = top_inverse[0]
    forward_leaf, leaf_updates = leaf_forward(top_total, rhs_leaf, blocks, inverses, leaf_struct)
    own_update = lax.psum_scatter(leaf_updates, "sn", scatter_dimension=0, tiled=True)
    top_source = rhs_top[0] - own_update[0]
    keep_row = lax.dynamic_index_in_dim(keep, my_index, 0, False)
    row_blocks = lax.all_to_all(top_cols, "sn", split_axis=0, concat_axis=1, tiled=True)
    masked_rows = row_blocks[0] * keep_row[:, None, None]
    forward_own = forward_by_rows(
        top_source,
        masked_rows,
        own_inverse,
        my_level,
        levels,
        lambda stacked: lax.all_gather(stacked, "sn", axis=0, tiled=True),
    )
    backward_own = backward_by_rows(
        forward_own,
        masked_rows,
        own_inverse,
        my_level,
        levels,
        lambda stacked: lax.psum_scatter(stacked, "sn", scatter_dimension=0, tiled=True),
    )
    all_top = lax.all_gather(backward_own[None], "sn", axis=0, tiled=True)
    leaf_solution = leaf_backward(forward_leaf, blocks, inverses, leaf_struct, all_top)
    return (leaf_solution, backward_own[None])


def solution(mesh):
    return jax.shard_map(
        local,
        mesh=mesh,
        in_specs=(
            P("sn", "rhs", None),
            P("sn", "rhs", None),
            P("sn", None, "rhs", None),
            P("sn", "rhs", None),
            P("sn", None),
            P(None, "sn", "rhs", None),
            P("sn", "rhs", None),
        ),
        out_specs=(P("sn", "rhs", None), P("sn", "rhs", None)),
        check_vma=False,
    )
```

profile of v0, /device:TPU:1, one launch (start us, length us, event | category | flops | bytes accessed | tf_op | source)
XLA Modules:
  0.0 1077.8 jit_solution(17331218211384969366)
XLA Ops:
  9.5 34.2 %all-gather.18.cloned.1.call-done = f32[32,128,128]{2,1,0:T(8,128)} async-done(((f32[32,32,128]{2,1,0:T(8,128)}), f32[32,128,128]{2,1,0:T(8,128)}) %all-gather.18.cloned.1.call-update) | async-done | bytes 2097168 | tf_op jit(solution)/shard_map/all_gather | solution.py:113
  43.7 67.4 %all-gather.16.cloned.1.call-done = f32[32,3,128,128]{3,2,1,0:T(8,128)} async-done(((f32[32,3,32,128]{3,2,1,0:T(8,128)}), f32[32,3,128,128]{3,2,1,0:T(8,128)}) %all-gather.16.cloned.1.call-update) | async-done | bytes 6291472 | tf_op jit(solution)/shard_map/all_gather | solution.py:112
  111.4 100.6 %while.30 = (s32[]{:T(128)}, f32[64,64,128]{2,1,0:T(8,128)S(1)}, f32[32,64,128]{2,1,0:T(8,128)S(1)}, s32[32,3]{1,0:T(8,128)S(1)}, f32[32,3,128,128]{3,2,1,0:T(8,...) while((s32[]{:T(128)}, f32[64,64,128]{2,1,0:T(8,128)S(1)}, ...), condition=%wide.region_2.3_spmd, body=%wide.region_0.2_spmd.sunk | while | flops 50364424 | bytes 821373 | solution.py:51
  121.9 1.3 convolution_bitcast_fusion.9
  137.7 1.3 convolution_bitcast_fusion.9
  214.5 9.0 all_gather.32
  223.5 10.7 all-to-all-start
  234.3 55.7 %reduce-scatter.7.cloned.1.call-done = f32[1,64,128]{2,1,0:T(8,128)} async-done(((f32[32,64,128]{2,1,0:T(8,128)}), f32[1,64,128]{2,1,0:T(8,128)}) %reduce-scatter.7.cloned.1.call-update) | async-done | bytes 32784 | tf_op jit(solution)/shard_map/reduce_scatter | solution.py:124
  293.6 42.9 %all-gather.22.cloned.1.call-done = f32[2048,128]{1,0:T(8,128)} async-done(((f32[64,128]{1,0:T(8,128)}), f32[2048,128]{1,0:T(8,128)}) %all-gather.22.cloned.1.call-update) | async-done | bytes 1048592 | tf_op jit(solution)/shard_map/all_gather | solution.py:135
  336.6 3.6 fusion.36
  341.8 41.2 %all-gather.24.cloned.1.call-done = f32[2048,128]{1,0:T(8,128)} async-done(((f32[64,128]{1,0:T(8,128)}), f32[2048,128]{1,0:T(8,128)}) %all-gather.24.cloned.1.call-update) | async-done | bytes 1048592 | tf_op jit(solution)/shard_map/all_gather | solution.py:135
  383.0 3.6 fusion.35
  388.2 41.2 %all-gather.26.cloned.1.call-done = f32[2048,128]{1,0:T(8,128)} async-done(((f32[64,128]{1,0:T(8,128)}), f32[2048,128]{1,0:T(8,128)}) %all-gather.26.cloned.1.call-update) | async-done | bytes 1048592 | tf_op jit(solution)/shard_map/all_gather | solution.py:135
  429.4 3.6 fusion.34
  434.6 41.2 %all-gather.28.cloned.1.call-done = f32[2048,128]{1,0:T(8,128)} async-done(((f32[64,128]{1,0:T(8,128)}), f32[2048,128]{1,0:T(8,128)}) %all-gather.28.cloned.1.call-update) | async-done | bytes 1048592 | tf_op jit(solution)/shard_map/all_gather | solution.py:135
  475.9 3.6 fusion.33
  481.3 41.0 %all-gather.30.cloned.1.call-done = f32[2048,128]{1,0:T(8,128)} async-done(((f32[64,128]{1,0:T(8,128)}), f32[2048,128]{1,0:T(8,128)}) %all-gather.30.cloned.1.call-update) | async-done | bytes 1048592 | tf_op jit(solution)/shard_map/all_gather | solution.py:135
  522.3 3.6 fusion.32
  526.3 2.4 fusion.31
  528.8 75.1 %reduce-scatter.9.cloned.1.call-done = f32[1,64,128]{2,1,0:T(8,128)} async-done(((f32[32,64,128]{2,1,0:T(8,128)}), f32[1,64,128]{2,1,0:T(8,128)}) %reduce-scatter.9.cloned.1.call-update) | async-done | bytes 32784 | tf_op jit(solution)/shard_map/reduce_scatter | solution.py:143
  604.9 2.4 fusion.30
  607.4 77.8 %reduce-scatter.11.cloned.1.call-done = f32[1,64,128]{2,1,0:T(8,128)} async-done(((f32[32,64,128]{2,1,0:T(8,128)}), f32[1,64,128]{2,1,0:T(8,128)}) %reduce-scatter.11.cloned.1.call-update) | async-done | bytes 32784 | tf_op jit(solution)/shard_map/reduce_scatter | solution.py:143
  686.1 2.4 fusion.29
  688.6 77.6 %reduce-scatter.13.cloned.1.call-done = f32[1,64,128]{2,1,0:T(8,128)} async-done(((f32[32,64,128]{2,1,0:T(8,128)}), f32[1,64,128]{2,1,0:T(8,128)}) %reduce-scatter.13.cloned.1.call-update) | async-done | bytes 32784 | tf_op jit(solution)/shard_map/reduce_scatter | solution.py:143
  767.2 2.4 fusion.28
  769.6 77.8 %reduce-scatter.15.cloned.1.call-done = f32[1,64,128]{2,1,0:T(8,128)} async-done(((f32[32,64,128]{2,1,0:T(8,128)}), f32[1,64,128]{2,1,0:T(8,128)}) %reduce-scatter.15.cloned.1.call-update) | async-done | bytes 32784 | tf_op jit(solution)/shard_map/reduce_scatter | solution.py:143
  848.4 2.4 fusion.27
  850.9 77.5 %reduce-scatter.17.cloned.1.call-done = f32[1,64,128]{2,1,0:T(8,128)} async-done(((f32[32,64,128]{2,1,0:T(8,128)}), f32[1,64,128]{2,1,0:T(8,128)}) %reduce-scatter.17.cloned.1.call-update) | async-done | bytes 32784 | tf_op jit(solution)/shard_map/reduce_scatter | solution.py:143
  928.4 1.6 convolution_select_fusion
  930.0 45.2 %all-gather.32.cloned.1.call-done = f32[2048,128]{1,0:T(8,128)} async-done(((f32[64,128]{1,0:T(8,128)}), f32[2048,128]{1,0:T(8,128)}) %all-gather.32.cloned.1.call-update) | async-done | bytes 1048592 | tf_op jit(solution)/shard_map/all_gather | solution.py:145
  975.2 1.5 concatenate.3
  976.6 93.5 %while.31 = (s32[]{:T(128)}, f32[64,64,128]{2,1,0:T(8,128)S(1)}, f32[32,64,128]{2,1,0:T(8,128)S(1)}, s32[32,3]{1,0:T(8,128)S(1)}, f32[32,3,128,128]{3,2,1,0:T(8,...) while((s32[]{:T(128)}, f32[64,64,128]{2,1,0:T(8,128)S(1)}, ...), condition=%wide.region_10.11_spmd, body=%wide.region_9.10_spmd.sunk | while | flops 50365472 | bytes 693510 | solution.py:78
  (395 shorter events, 204.5 us)
Async XLA Ops:
  7.2 2.3 copy-start.10
  7.2 36.5 %all-gather.18.cloned.1.call-start = ((), (), s32[]{:S(2)}) async-start(), calls=%async_computation.8 | async-start | bytes 2621440 | tf_op jit(solution)/shard_map/all_gather | solution.py:113
  7.9 103.2 %all-gather.16.cloned.1.call-start = ((), (), s32[]{:S(2)}) async-start(), calls=%async_computation.7 | async-start | bytes 7864320 | tf_op jit(solution)/shard_map/all_gather | solution.py:112
  8.7 214.9 %all-gather.20.cloned.1.call-start = ((), (), s32[]{:S(2)}) async-start(), calls=%async_computation.10 | async-start | bytes 2621440 | tf_op jit(solution)/shard_map/all_gather | solution.py:114
  9.4 280.6 %reduce-scatter.7.cloned.1.call-start = ((), (), s32[]{:S(2)}) async-start(), calls=%async_computation.9 | async-start | bytes 1081344 | tf_op jit(solution)/shard_map/reduce_scatter | solution.py:124
  212.0 2.5 copy-start.9
  223.5 66.4 %copy-start.8 = (f32[1,64,128]{2,1,0:T(8,128)S(1)}, f32[1,64,128]{2,1,0:T(8,128)}, u32[]{:S(2)}) copy-start(f32[1,64,128]{2,1,0:T(8,128)} %param.12) | copy-start | bytes 98308
  223.5 70.1 %all-to-all-start = ((f32[32,1,128,128]{3,2,1,0:T(8,128)}), f32[32,1,128,128]{3,2,1,0:T(8,128)S(1)}, u32[]{:S(2)}, u32[]{:S(2)}) async-start(f32[32,1,128,128]{3,2,1,0:T(8,128)} %all-gather.20.cloned.1.call-done), calls=%async_computation.1 | async-start | bytes 4194304 | tf_op jit(solution)/shard_map/all_to_all | solution.py:127
  234.2 102.3 %all-gather.22.cloned.1.call-start = ((), (), s32[]{:S(2)}) async-start(), calls=%async_computation.16 | async-start | bytes 1081344 | tf_op jit(solution)/shard_map/all_gather | solution.py:135
  291.6 48.6 %copy-start.4 = (f32[64,128]{1,0:T(8,128)S(1)}, f32[64,128]{1,0:T(8,128)}, u32[]{:S(2)}) copy-start(f32[64,128]{1,0:T(8,128)} %convolution_select_fusion.11) | copy-start | bytes 98308
  291.6 91.4 %all-gather.24.cloned.1.call-start = ((), (), s32[]{:S(2)}) async-start(), calls=%async_computation.17 | async-start | bytes 1081344 | tf_op jit(solution)/shard_map/all_gather | solution.py:135
  341.0 45.6 %copy-start.1 = (f32[64,128]{1,0:T(8,128)S(1)}, f32[64,128]{1,0:T(8,128)}, u32[]{:S(2)}) copy-start(f32[64,128]{1,0:T(8,128)} %convolution_select_fusion.10) | copy-start | bytes 98308
  341.0 88.4 %all-gather.26.cloned.1.call-start = ((), (), s32[]{:S(2)}) async-start(), calls=%async_computation.18 | async-start | bytes 1081344 | tf_op jit(solution)/shard_map/all_gather | solution.py:135
  387.4 45.6 %copy-start.2 = (f32[64,128]{1,0:T(8,128)S(1)}, f32[64,128]{1,0:T(8,128)}, u32[]{:S(2)}) copy-start(f32[64,128]{1,0:T(8,128)} %convolution_select_fusion.9) | copy-start | bytes 98308
  387.5 88.4 %all-gather.28.cloned.1.call-start = ((), (), s32[]{:S(2)}) async-start(), calls=%async_computation.19 | async-start | bytes 1081344 | tf_op jit(solution)/shard_map/all_gather | solution.py:135
  433.9 45.6 %copy-start.3 = (f32[64,128]{1,0:T(8,128)S(1)}, f32[64,128]{1,0:T(8,128)}, u32[]{:S(2)}) copy-start(f32[64,128]{1,0:T(8,128)} %convolution_select_fusion.8) | copy-start | bytes 98308
  433.9 88.4 %all-gather.30.cloned.1.call-start = ((), (), s32[]{:S(2)}) async-start(), calls=%async_computation.20 | async-start | bytes 1081344 | tf_op jit(solution)/shard_map/all_gather | solution.py:135
  480.3 45.6 %copy-start = (f32[64,128]{1,0:T(8,128)S(1)}, f32[64,128]{1,0:T(8,128)}, u32[]{:S(2)}) copy-start(f32[64,128]{1,0:T(8,128)} %convolution_select_fusion.7) | copy-start | bytes 98308
  480.3 123.6 %reduce-scatter.9.cloned.1.call-start = ((), (), s32[]{:S(2)}) async-start(), calls=%async_computation.11 | async-start | bytes 1081344 | tf_op jit(solution)/shard_map/reduce_scatter | solution.py:143
  528.8 156.4 %reduce-scatter.11.cloned.1.call-start = ((), (), s32[]{:S(2)}) async-start(), calls=%async_computation.12 | async-start | bytes 1081344 | tf_op jit(solution)/shard_map/reduce_scatter | solution.py:143
  604.9 80.3 %copy-start.5 = (f32[1,64,128]{2,1,0:T(8,128)S(1)}, f32[1,64,128]{2,1,0:T(8,128)}, u32[]{:S(2)}) copy-start(f32[1,64,128]{2,1,0:T(8,128)} %reduce-scatter.9.cloned.1.call-done) | copy-start | bytes 98308
  607.3 158.9 %reduce-scatter.13.cloned.1.call-start = ((), (), s32[]{:S(2)}) async-start(), calls=%async_computation.13 | async-start | bytes 1081344 | tf_op jit(solution)/shard_map/reduce_scatter | solution.py:143
  686.1 80.1 %copy-start.6 = (f32[1,64,128]{2,1,0:T(8,128)S(1)}, f32[1,64,128]{2,1,0:T(8,128)}, u32[]{:S(2)}) copy-start(f32[1,64,128]{2,1,0:T(8,128)} %reduce-scatter.11.cloned.1.call-done) | copy-start | bytes 98308
  688.5 158.9 %reduce-scatter.15.cloned.1.call-start = ((), (), s32[]{:S(2)}) async-start(), calls=%async_computation.14 | async-start | bytes 1081344 | tf_op jit(solution)/shard_map/reduce_scatter | solution.py:143
  769.6 158.8 %reduce-scatter.17.cloned.1.call-start = ((), (), s32[]{:S(2)}) async-start(), calls=%async_computation.15 | async-start | bytes 1081344 | tf_op jit(solution)/shard_map/reduce_scatter | solution.py:143
  848.4 80.0 %copy-start.7 = (f32[1,64,128]{2,1,0:T(8,128)S(1)}, f32[1,64,128]{2,1,0:T(8,128)}, u32[]{:S(2)}) copy-start(f32[1,64,128]{2,1,0:T(8,128)} %reduce-scatter.15.cloned.1.call-done) | copy-start | bytes 98308
  850.8 124.3 %all-gather.32.cloned.1.call-start = ((), (), s32[]{:S(2)}) async-start(), calls=%async_computation.21 | async-start | bytes 1081344 | tf_op jit(solution)/shard_map/all_gather | solution.py:145
Sparse Core Ops, SparseCore 0:
  9.6 34.0 all-gather.17
  45.4 65.7 all-gather.15
  112.8 31.4 all-gather.19
  213.3 76.6 reduce-scatter.6
  292.6 43.8 all-gather.21
  341.1 41.7 all-gather.23
  387.6 41.7 all-gather.25
  434.0 41.7 all-gather.27
  480.5 41.7 all-gather.29
  528.9 75.0 reduce-scatter.8
  608.0 77.0 reduce-scatter.10
  689.1 77.0 reduce-scatter.12
  770.3 77.1 reduce-scatter.14
  851.4 77.0 reduce-scatter.16
  931.1 44.0 all-gather.31
where the time goes:
time: 1080 us
  waiting for transfers between devices  798 us (74%)
  matrix products  189 us (18%)
  other arithmetic  25.3 us (2%)
  local copies, waits for them, and re-layouts  23 us (2%)
  between operations  18.4 us (2%)
  starting transfers between devices  11.5 us (1%)
    reduce_scatter x5, waiting for transfers between devices, local(): lax.psum_scatter(stacked, 'sn', scatter_dimension=0, tiled=True)  386 us
    all_gather x5, waiting for transfers between devices, local(): lax.all_gather(stacked, 'sn', axis=0, tiled=True)  208 us
    all_gather x1, waiting for transfers between devices, local(): lax.all_gather(leaf_blocks, 'rhs', axis=2, tiled=True)  67.4 us
    reduce_scatter x1, waiting for transfers between devices, local(): lax.psum_scatter(leaf_updates, 'sn', scatter_dimension=0, tiled=True)  55.7 us
    all_gather x1, waiting for transfers between devices, local(): all_top = lax.all_gather(backward_own[None], 'sn', axis=0, tiled=True)  45.2 us
    dot_general x32, matrix products, advance(): jnp.einsum('ck,rik->rci', solved, lax.dynamic_index_in_dim(blocks, positi...  41.9 us
    dot_general x32, matrix products, retreat(): jnp.einsum('rci,rik->ck', ancestors, lax.dynamic_index_in_dim(blocks, pos...  39.4 us
    dot_general x32, matrix products, advance(): jnp.einsum('ck,ik->ci', source, lax.dynamic_index_in_dim(inverses, positi...  35.3 us
  transfers between devices with their start and end apart: 16, of which 14 were waited for; matrix products, arithmetic and copies ran while one was open for 10% of the time, Pallas kernels for 0%

commit v1 on v0

v1 whole, which is shorter than its diff:
```python
import functools

import jax
import jax.numpy as jnp
from jax import lax
from jax.experimental import pallas as pl
from jax.experimental.pallas import tpu as pltpu
from jax.sharding import PartitionSpec as P

MESH = pl.DeviceIdType.MESH
f32 = jnp.float32
bf16 = jnp.bfloat16

CHUNK = 2
AHEAD = 2
TOP_Z, TOP_GROUP, TOP_SOLVER = 3, 6, 10


def split(x):
    high = x.astype(bf16)
    return high, (x - high.astype(f32)).astype(bf16)


def dot3(x, w, transposed):
    dims = (((1,), (1 if transposed else 0,)), ((), ()))
    dot = functools.partial(lax.dot_general, dimension_numbers=dims, preferred_element_type=f32)
    x_high, x_low = split(x)
    w_high, w_low = split(w)
    return dot(x_high, w_high) + (dot(x_high, w_low) + dot(x_low, w_high))


def trailing(q):
    count = 0
    while (q >> count) & 1:
        count += 1
    return count


def kernel(
    slot_ref, rl, rt, lb, ld, tb, td,
    o_leaf, o_top,
    acc, blk, dinv, fwd, zbuf, tg, rtop, part, contrib, gathered, upper, xs, xpath, zown, ftop,
    s_direct, s_relay, r_direct, r_relay,
    s_top, r_top, s_rt, r_rt, s_grp, r_grp, s_up, r_up, s_part, r_part, s_con, r_con, s_x, r_x, s_z, r_z,
    l_sem,
):
    leaf, cols, w = rl.shape
    quarter = w // 4
    half = quarter // 2
    cc = cols // 4
    chunks = leaf // CHUNK
    sn, z = lax.axis_index("sn"), lax.axis_index("rhs")
    g, c = sn // 4, sn % 4
    zr, zl, zo = lax.rem(z + 1, 4), lax.rem(z + 3, 4), lax.rem(z + 2, 4)
    solver = 2 * c
    is_solver = g == solver
    my_cols = pl.ds(pl.multiple_of(c * cc, cc), cc)

    def mate(i):
        return 4 * g + lax.rem(c + i, 4)

    def classmate(i):
        return 4 * lax.rem(g + i, 8) + c

    def remote(src, dst, ssem, rsem, device):
        return pltpu.make_async_remote_copy(
            src_ref=src, dst_ref=dst, send_sem=ssem, recv_sem=rsem, device_id=device, device_id_type=MESH
        )

    barrier = pltpu.get_barrier_semaphore()
    for i in range(1, 4):
        pl.semaphore_signal(barrier, inc=1, device_id=(sn, lax.rem(z + i, 4)), device_id_type=MESH)
        pl.semaphore_signal(barrier, inc=1, device_id=(mate(i), z), device_id_type=MESH)
    for i in range(1, 8):
        pl.semaphore_signal(barrier, inc=1, device_id=(classmate(i), z), device_id_type=MESH)

    locals_ = [
        pltpu.make_async_copy(rl, acc.at[pl.ds(0, leaf)], l_sem.at[0]),
        pltpu.make_async_copy(lb, blk.at[:, :, z], l_sem.at[1]),
        pltpu.make_async_copy(ld, dinv.at[:, z], l_sem.at[2]),
        pltpu.make_async_copy(td.at[0], tg.at[c, 0, z], l_sem.at[3]),
        pltpu.make_async_copy(rt.at[0, my_cols], rtop.at[c], l_sem.at[4]),
    ]
    ancestors = [(sn >> l) * (1 << l) + ((1 << l) - 1) for l in range(6)]
    for l in range(1, 6):
        locals_.append(pltpu.make_async_copy(tb.at[ancestors[l], 0], tg.at[c, l, z], l_sem.at[4 + l]))
    for copy in locals_:
        copy.start()
    acc[leaf:] = jnp.zeros((6, cols, w), f32)

    pl.semaphore_wait(barrier, 13)

    def direct(j, way):
        there = (sn, zr if way == 0 else zl)
        at = pl.ds(j * CHUNK, CHUNK)
        return [
            remote(lb.at[at], blk.at[at, :, z], s_direct.at[way, 0], r_direct.at[way, 0, j], there),
            remote(ld.at[at], dinv.at[at, z], s_direct.at[way, 1], r_direct.at[way, 1, j], there),
        ]

    def relay(j, way):
        there = (sn, zr if way == 0 else zl)
        owner = zl if way == 0 else zr
        at = pl.ds(j * CHUNK, CHUNK)
        rows = pl.ds(0 if way == 0 else half, half)
        b, d = blk.at[at, :, owner, rows], dinv.at[at, owner, rows]
        return [
            remote(b, b, s_relay.at[way, 0], r_relay.at[way, 0, j], there),
            remote(d, d, s_relay.at[way, 1], r_relay.at[way, 1, j], there),
        ]

    def direct_start(j):
        for way in range(2):
            for copy in direct(j, way):
                copy.start()

    direct_start(0)

    def top_z(i):
        there = (sn, lax.rem(z + i, 4))
        copies = [remote(td.at[0], tg.at[c, 0, z], s_top.at[i], r_top.at[i], there)]
        for l in range(1, 6):
            copies.append(remote(tb.at[ancestors[l], 0], tg.at[c, l, z], s_top.at[i], r_top.at[i], there))
        return copies

    def top_z_all(i):
        src = lax.rem(z + 4 - i, 4)
        view = tg.at[c, :, src]
        return remote(view, view, s_top.at[i], r_top.at[i], (sn, lax.rem(z + i, 4)))

    for i in range(1, 4):
        for copy in top_z(i):
            copy.start()

    def share_rhs(i):
        to = lax.rem(c + i, 4)
        return remote(
            rt.at[0, pl.ds(pl.multiple_of(to * cc, cc), cc)], rtop.at[c], s_rt.at[i], r_rt.at[i], (mate(i), z)
        )

    for i in range(1, 4):
        share_rhs(i).start()
    for j in range(1, AHEAD):
        direct_start(j)

    def share_group(i):
        return remote(tg.at[c], tg.at[c], s_grp.at[i], r_grp.at[i], (mate(i), z))

    def share_upper():
        there = (4 * solver + c, z)
        return [
            remote(tg.at[3, 0], upper.at[g, 0], s_up, r_up.at[g], there),
            remote(tg.at[3, pl.ds(3, 3)], upper.at[g, pl.ds(1, 3)], s_up, r_up.at[g], there),
        ]

    def upper_all(at):
        return remote(upper.at[at], upper.at[at], s_up, r_up.at[at], (4 * solver + c, z))

    for copy in locals_:
        copy.wait()

    def leaf_block(s):
        return blk[s].reshape(3 * w, w), dinv[s].reshape(w, w)

    def forward_step(s):
        b, d = leaf_block(s)
        solved = dot3(acc[s], d, True)
        fwd[s] = solved
        out = dot3(solved, b, True)
        acc[s + 1] = acc[s + 1] - out[:, :w]
        first, second = slot_ref[s, 1], slot_ref[s, 2]
        out1, out2 = out[:, w : 2 * w], out[:, 2 * w :]

        def push(t):
            m1 = (first == t).astype(f32)
            m2 = (second == t).astype(f32)
            acc[t] = acc[t] - (m1 * out1 + m2 * out2)

        for t in range(2, leaf + 6):
            push(t)

    def turn(j, carry):
        @pl.when(j + AHEAD < chunks)
        def _():
            direct_start(j + AHEAD)

        @pl.when(j < chunks)
        def _():
            for way in range(2):
                for copy in direct(j, way):
                    copy.wait_recv()
                for copy in relay(j, way):
                    copy.start()

        @pl.when(j == min(TOP_Z, chunks))
        def _():
            for i in range(1, 4):
                top_z_all(i).wait_recv()
            for i in range(1, 4):
                share_group(i).start()

        @pl.when(j == min(TOP_GROUP, chunks))
        def _():
            for i in range(1, 4):
                share_group(i).wait_recv()

            @pl.when(jnp.logical_not(is_solver))
            def _():
                for copy in share_upper():
                    copy.start()

        @pl.when(j >= 1)
        def _():
            for way in range(2):
                for copy in relay(j - 1, way):
                    copy.wait_recv()
            for i in range(CHUNK):
                forward_step((j - 1) * CHUNK + i)

        return carry

    lax.fori_loop(0, chunks + 1, turn, 0)

    def share_part(i):
        to = lax.rem(c + i, 4)
        return remote(
            acc.at[pl.ds(leaf, 6), pl.ds(pl.multiple_of(to * cc, cc), cc)],
            part.at[c],
            s_part.at[i],
            r_part.at[i],
            (mate(i), z),
        )

    for i in range(1, 4):
        share_part(i).start()
    part[c] = acc[pl.ds(leaf, 6), my_cols]

    for i in range(1, 4):
        share_rhs(i).wait_recv()
        share_part(i).wait_recv()

    def top_block(m, l):
        return tg[m, l].reshape(w, w)

    def top_stack(m):
        return tg[m, 2:6].reshape(4 * w, w)

    path = part[0] + part[1] + part[2] + part[3]
    f0 = dot3(path[0] + rtop[0], top_block(0, 0), True)
    f1 = dot3(path[1] + rtop[1] - dot3(f0, top_block(0, 1), True), top_block(1, 0), True)
    f2 = dot3(rtop[2], top_block(2, 0), True)
    out = dot3(f0, top_stack(0), True) + dot3(f1, top_stack(1), True) + dot3(f2, top_stack(2), True)
    ftop[0], ftop[1], ftop[2] = f0, f1, f2
    last = 4 * g + 3
    above = [(last + 1) % (1 << l) == 0 for l in range(6)] + [last + 1 == 64]
    for l in range(2, 6):
        mine = above[l]
        if l < 5:
            mine = jnp.logical_and(mine, jnp.logical_not(above[l + 1]))
        contrib[l - 2] = path[l] + mine.astype(f32) * rtop[3] - out[:, (l - 2) * w : (l - 1) * w]

    def share_contrib():
        return remote(contrib, gathered.at[g], s_con, r_con.at[g], (4 * solver + c, z))

    def contrib_from(at):
        return remote(gathered.at[at], gathered.at[at], s_con, r_con.at[at], (4 * solver + c, z))

    def share_x(i):
        to = lax.rem(g + i, 8)
        return remote(xs.at[to], xpath, s_x.at[i], r_x, (classmate(i), z))

    @pl.when(jnp.logical_not(is_solver))
    def _():
        share_contrib().start()

    @pl.when(is_solver)
    def _():
        upper[g, 0] = tg[3, 0]
        upper[g, 1:4] = tg[3, 3:6]
        gathered[g] = contrib[...]
        for i in range(1, 8):
            at = lax.rem(g + i, 8)
            upper_all(at).wait_recv()
            contrib_from(at).wait_recv()

        def upper_block(q, slot):
            return upper[q, slot].reshape(w, w)

        spans = [range(q + 1 - (1 << trailing(q)), q) for q in range(8)]
        order = sorted(range(8), key=lambda q: (trailing(q), q))
        forward = {}
        for q in order:
            level = trailing(q)
            source = gathered[q, level]
            for below in spans[q]:
                source = source + gathered[below, level]
            for below in spans[q]:
                source = source - dot3(forward[below], upper_block(below, level), True)
            forward[q] = dot3(source, upper_block(q, 0), True)
        solved = {}
        for q in reversed(order):
            source = forward[q]
            for up in range(q + 1, 8):
                if q in spans[up]:
                    source = source - dot3(solved[up], upper_block(q, trailing(up)), False)
            solved[q] = dot3(source, upper_block(q, 0), False)
        for to in range(8):
            for level in range(4):
                q = (to >> level) * (1 << level) + (1 << level) - 1
                if trailing(q) == level:
                    xs[to, level] = solved[q]
                else:
                    xs[to, level] = jnp.zeros((cc, w), f32)
        for i in range(1, 8):
            share_x(i).start()
        xpath[...] = xs[g]

    @pl.when(jnp.logical_not(is_solver))
    def _():
        remote(xpath, xpath, s_x.at[0], r_x, (4 * solver + c, z)).wait_recv()

    across = jnp.concatenate([xpath[0], xpath[1], xpath[2], xpath[3]], axis=1)
    x1 = dot3(ftop[1] - dot3(across, top_stack(1), False), top_block(1, 0), False)
    x2 = dot3(ftop[2] - dot3(across, top_stack(2), False), top_block(2, 0), False)
    x0 = dot3(
        ftop[0] - dot3(across, top_stack(0), False) - dot3(x1, top_block(0, 1), False), top_block(0, 0), False
    )
    zown[0], zown[1], zown[6] = x0, x1, x2
    zown[2:6] = xpath[...]

    def share_z(i):
        return remote(zown, zbuf.at[pl.ds(leaf, 7), my_cols], s_z.at[i], r_z.at[i], (mate(i), z))

    def z_from(i):
        src = lax.rem(c + 4 - i, 4)
        view = zbuf.at[pl.ds(leaf, 7), pl.ds(pl.multiple_of(src * cc, cc), cc)]
        return remote(zown, view, s_z.at[i], r_z.at[i], (mate(i), z))

    for i in range(1, 4):
        share_z(i).start()
    zbuf[pl.ds(leaf, 7), my_cols] = zown[...]
    for i in range(1, 4):
        z_from(i).wait_recv()

    def backward(offset, carry):
        s = leaf - 1 - offset
        b, d = leaf_block(s)
        z_at = jnp.concatenate([zbuf[s + 1], zbuf[slot_ref[s, 1]], zbuf[slot_ref[s, 2]]], axis=1)
        zbuf[s] = dot3(fwd[s] - dot3(z_at, b, False), d, False)
        return carry

    lax.fori_loop(0, leaf, backward, 0)

    level = sum(jnp.where((sn + 1) % (1 << l) == 0, 1, 0) for l in range(1, 6))
    place = jnp.where(c == 2, 6, level)
    outs = [
        pltpu.make_async_copy(zbuf.at[pl.ds(0, leaf)], o_leaf, l_sem.at[0]),
        pltpu.make_async_copy(zbuf.at[leaf + place], o_top.at[0], l_sem.at[1]),
    ]
    for copy in outs:
        copy.start()

    whole = pl.ds(0, leaf)
    for way in range(2):
        there = (sn, zr if way == 0 else zl)
        owner = zl if way == 0 else zr
        rows = pl.ds(0 if way == 0 else half, half)
        remote(lb, blk.at[:, :, z], s_direct.at[way, 0], r_direct.at[way, 0, 0], there).wait_send()
        remote(ld, dinv.at[:, z], s_direct.at[way, 1], r_direct.at[way, 1, 0], there).wait_send()
        b, d = blk.at[whole, :, owner, rows], dinv.at[whole, owner, rows]
        remote(b, b, s_relay.at[way, 0], r_relay.at[way, 0, 0], there).wait_send()
        remote(d, d, s_relay.at[way, 1], r_relay.at[way, 1, 0], there).wait_send()
    for i in range(1, 4):
        top_z_all(i).wait_send()
        share_rhs(i).wait_send()
        share_group(i).wait_send()
        share_part(i).wait_send()
        share_z(i).wait_send()

    @pl.when(jnp.logical_not(is_solver))
    def _():
        upper_all(g).wait_send()
        share_contrib().wait_send()

    @pl.when(is_solver)
    def _():
        for i in range(1, 8):
            share_x(i).wait_send()

    for copy in outs:
        copy.wait()


def call(rl, rt, lb, ld, slots, tb, td):
    leaf, cols, w = rl.shape
    cc, quarter, chunks = cols // 4, w // 4, leaf // CHUNK
    any_spec = pl.BlockSpec(memory_space=pl.ANY)
    dma = pltpu.SemaphoreType.DMA
    return pl.pallas_call(
        kernel,
        out_shape=(jax.ShapeDtypeStruct(rl.shape, f32), jax.ShapeDtypeStruct(rt.shape, f32)),
        in_specs=[pl.BlockSpec(memory_space=pltpu.SMEM)] + [any_spec] * 6,
        out_specs=(any_spec, any_spec),
        scratch_shapes=[
            pltpu.VMEM((leaf + 6, cols, w), f32),
            pltpu.VMEM((leaf, 3, 4, quarter, w), f32),
            pltpu.VMEM((leaf, 4, quarter, w), f32),
            pltpu.VMEM((leaf, cols, w), f32),
            pltpu.VMEM((leaf + 7, cols, w), f32),
            pltpu.VMEM((4, 6, 4, quarter, w), f32),
            pltpu.VMEM((4, cc, w), f32),
            pltpu.VMEM((4, 6, cc, w), f32),
            pltpu.VMEM((4, cc, w), f32),
            pltpu.VMEM((8, 4, cc, w), f32),
            pltpu.VMEM((8, 4, 4, quarter, w), f32),
            pltpu.VMEM((8, 4, cc, w), f32),
            pltpu.VMEM((4, cc, w), f32),
            pltpu.VMEM((7, cc, w), f32),
            pltpu.VMEM((3, cc, w), f32),
            dma((2, 2)), dma((2, 2)), dma((2, 2, chunks)), dma((2, 2, chunks)),
            dma((4,)), dma((4,)), dma((4,)), dma((4,)), dma((4,)), dma((4,)),
            dma, dma((8,)), dma((4,)), dma((4,)), dma, dma((8,)), dma((8,)), dma, dma((4,)), dma((4,)),
            dma((10,)),
        ],
        compiler_params=pltpu.CompilerParams(
            collective_id=0, has_side_effects=True, vmem_limit_bytes=60 * 1024 * 1024
        ),
        name="substitution",
    )(slots, rl, rt, lb, ld, tb, td)


def local(rhs_leaf, rhs_top, leaf_blocks, leaf_dinv, leaf_struct, top_blocks, top_dinv):
    leaf = rhs_leaf.shape[0]
    top = leaf_struct - leaf
    level = sum(((top + 1) % (1 << l) == 0).astype(jnp.int32) for l in range(1, 6))
    slots = jnp.where(top < 0, leaf_struct, leaf + level)
    return call(rhs_leaf, rhs_top, leaf_blocks, leaf_dinv, slots, top_blocks, top_dinv)


def solution(mesh):
    return jax.shard_map(
        local,
        mesh=mesh,
        in_specs=(
            P("sn", "rhs", None),
            P("sn", "rhs", None),
            P("sn", None, "rhs", None),
            P("sn", "rhs", None),
            P("sn", None),
            P(None, "sn", "rhs", None),
            P("sn", "rhs", None),
        ),
        out_specs=(P("sn", "rhs", None), P("sn", "rhs", None)),
        check_vma=False,
    )
```

time: 1080 us -> 132 us (0.12)
  waiting for transfers between devices: 798 us -> 0 us
  matrix products: 189 us -> 0 us
  Pallas kernels: 0 us -> 125 us
  other arithmetic: 25.3 us -> 1.33 us
  local copies, waits for them, and re-layouts: 23 us -> 3.8 us
  between operations: 18.4 us -> 0.65 us
  starting transfers between devices: 11.5 us -> 0 us
    reduce_scatter x6 -> x0, waiting for transfers between devices: 441 us -> none  [the longest x5 386 us: local(): lax.psum_scatter(stacked, 'sn', scatter_dimension=0, tiled=True)]
    all_gather x9 -> x0, waiting for transfers between devices: 354 us -> none  [the longest x5 208 us: local(): lax.all_gather(stacked, 'sn', axis=0, tiled=True)]
    dot_general x150 -> x0, matrix products: 189 us -> none  [the longest x32 41.9 us: advance(): jnp.einsum('ck,rik->rci', solved, lax.dynamic_index_in_dim(blocks, positi...]
    pallas_call x0 -> x1, Pallas kernels: none -> 125 us  [call(): pl.pallas_call(kernel, out_shape=(jax.ShapeDtypeStruct(rl.shape, f32), ja...]
    scatter-add x32 -> x0, other arithmetic: 21.6 us -> none  [advance(): updates = updates.at[targets].add(outgoing)]
    gather x32 -> x0, local copies, waits for them, and re-layouts: 17.8 us -> none  [retreat(): ancestors = jnp.take(solution_buffer, targets, axis=0)]
  transfers between devices with their start and end apart: 16 -> 0, of which waited for: 14 -> 0; matrix products, arithmetic and copies ran while one was open for 10% -> 0% of each run, Pallas kernels for 0% -> 0%
where the time goes in v1:
time: 132 us; the launch traced here: 131 us
  Pallas kernels  125 us (95%)
  local copies, waits for them, and re-layouts  3.8 us (3%)
  other arithmetic  1.33 us (1%)
    pallas_call x1, Pallas kernels, call(): pl.pallas_call(kernel, out_shape=(jax.ShapeDtypeStruct(rl.shape, f32), ja...  125 us
    unnamed x5, local copies, waits for them, and re-layouts  3.69 us

profile of v1, /device:TPU:1, one launch (start us, length us, event | category | flops | bytes accessed | tf_op | source)
XLA Modules:
  0.0 131.3 jit_solution(2698302794678228339)
XLA Ops:
  0.6 0.7 add_compare_fusion
  1.3 0.1 copy.16
  1.4 0.8 copy.17
  2.2 0.6 add_select_fusion.5.slot_ref
  2.8 125.5 %substitution.1 = (f32[32,64,128]{2,1,0:T(8,128)}, f32[1,64,128]{2,1,0:T(8,128)}) custom-call(s32[32,3]{1,0:T(8,128)} %add_select_fusion.5.slot_ref, f32[32,64,128]{2,1,0:T(8,128)} %rl.1, f32[1,64,128]{2,1,0:T(8,128)} %rt.1, f32[32,3,32,128]{3,2,1,0:T(8,128)} %lb.1, f32[32,32,128]{2,1,0:T(8,128)} %ld.1, f32[32,1,32,128]{3,2,1,0:T(8,128)} %tb.1, f32[1,32,128]{2,1,0:T(8,128)} %td.1), custom_call_target="tpu_custom_call" | custom-call | tf_op jit(solution)/shard_map/substitution/pallas_call | solution.py:399
  128.3 0.0 copy-start
  128.3 2.3 %copy.20 = f32[32,64,128]{2,1,0:T(8,128)} copy(f32[32,64,128]{2,1,0:T(8,128)} %get-tuple-element.4) | data formatting | bytes 2097152
  130.7 0.0 copy-done
  130.7 0.6 copy.21
Async XLA Ops:
  128.3 2.3 %copy-start = (f32[1,64,128]{2,1,0:T(8,128)S(1)}, f32[1,64,128]{2,1,0:T(8,128)}, u32[]{:S(2)}) copy-start(f32[1,64,128]{2,1,0:T(8,128)} %get-tuple-element.5) | copy-start | bytes 98308

commit v2 on v1

v2 whole, which is shorter than its diff:
```python
import functools

import jax
import jax.numpy as jnp
from jax import lax
from jax.experimental import pallas as pl
from jax.experimental.pallas import tpu as pltpu
from jax.sharding import PartitionSpec as P

MESH = pl.DeviceIdType.MESH
f32 = jnp.float32
bf16 = jnp.bfloat16

CHUNK = 2
AHEAD = 2
TOP_Z, TOP_GROUP, TOP_SOLVER = 3, 6, 10


def split(x):
    high = x.astype(bf16)
    return high, (x - high.astype(f32)).astype(bf16)


def dot3(x, w, transposed):
    dims = (((1,), (1 if transposed else 0,)), ((), ()))
    dot = functools.partial(lax.dot_general, dimension_numbers=dims, preferred_element_type=f32)
    x_high, x_low = split(x)
    w_high, w_low = split(w)
    return dot(x_high, w_high) + (dot(x_high, w_low) + dot(x_low, w_high))


def trailing(q):
    count = 0
    while (q >> count) & 1:
        count += 1
    return count


def kernel(
    st, rl, rt, lb, ld, tb, td,
    o_leaf, o_top,
    acc, rin, blk, dinv, fwd, zbuf, tg, rtop, part, contrib, gathered, upper, xs, xpath, zown, ftop, tout, stv, slot_ref,
    s_own, s_fwd, s_rhs, s_back, r_in, r_rhs, r_back,
    s_top, r_top, s_rt, r_rt, s_grp, r_grp, s_up, r_up, s_part, r_part, s_con, r_con, s_x, r_x, s_z, r_z, s_to, r_to,
    s_st, r_st, l_sem,
):
    leaf, cols, w = rl.shape
    quarter = w // 4
    cc = cols // 4
    chunks = leaf // CHUNK
    sn, z = lax.axis_index("sn"), lax.axis_index("rhs")
    g, c = sn // 4, sn % 4
    core, low = sn % 2, z // 2
    hub = core == low
    guest = jnp.logical_not(hub)
    role = jnp.where(hub, 0, 1)
    other, zm, zo = sn + 1 - 2 * core, z + 1 - 2 * (z % 2), 3 - z
    rows_of = (z, zo, zm, 3 - zm)
    place = 2 * (c // 2) + role
    solver = 2 * c
    is_solver = g == solver
    block = jnp.where(hub, z, zo)

    def at_cols(k):
        return pl.ds(pl.multiple_of(k * cc, cc), cc)

    my_cols = at_cols(place)

    def sibling(i):
        return 4 * g + lax.rem(c + i, 4)

    def classmate(i):
        return 4 * lax.rem(g + i, 8) + c

    def mate(k, i):
        to = lax.rem(k + i, 4)
        return to, (4 * g + 2 * (to // 2) + core, jnp.where(to % 2 == role, z, zo))

    def worker(k):
        return 4 * g + 2 * (k // 2) + low, (z if k % 2 == 0 else zo)

    def remote(src, dst, ssem, rsem, device):
        return pltpu.make_async_remote_copy(
            src_ref=src, dst_ref=dst, send_sem=ssem, recv_sem=rsem, device_id=device, device_id_type=MESH
        )

    barrier = pltpu.get_barrier_semaphore()

    def greet(device):
        pl.semaphore_signal(barrier, inc=1, device_id=device, device_id_type=MESH)

    for i in range(1, 4):
        greet((sibling(i), z))
    for i in range(4):
        greet((sibling(i), zo))
    greet((sn, zm))
    greet((sn, 3 - zm))
    for i in range(1, 8):
        greet((classmate(i), z))

    locals_ = [pltpu.make_async_copy(td.at[0], tg.at[c, 0, z], l_sem.at[0])]
    ancestors = [(sn >> l) * (1 << l) + ((1 << l) - 1) for l in range(6)]
    for l in range(1, 6):
        locals_.append(pltpu.make_async_copy(tb.at[ancestors[l], 0], tg.at[c, l, z], l_sem.at[l]))
    hub_locals = [
        pltpu.make_async_copy(rl, rin, l_sem.at[6]),
        pltpu.make_async_copy(lb, blk.at[:, :, z], l_sem.at[7]),
        pltpu.make_async_copy(ld, dinv.at[:, z], l_sem.at[8]),
        pltpu.make_async_copy(st, stv, l_sem.at[9]),
        pltpu.make_async_copy(rt.at[0, my_cols], rtop.at[c], l_sem.at[10]),
    ]
    for copy in locals_:
        copy.start()

    @pl.when(hub)
    def _():
        for copy in hub_locals:
            copy.start()

    def clear(t, carry):
        acc[t] = jnp.zeros((cols, w), f32)
        return carry

    lax.fori_loop(0, leaf + 6, clear, 0)
    pl.semaphore_wait(barrier, 16)

    def piece(j, k):
        at = pl.ds(j * CHUNK, CHUNK)
        return blk.at[at, :, rows_of[k]], dinv.at[at, rows_of[k]]

    def own(j, to, k, device):
        at = pl.ds(j * CHUNK, CHUNK)
        return [
            remote(lb.at[at], blk.at[at, :, z], s_own.at[to, 0], r_in.at[k, 0, j], device),
            remote(ld.at[at], dinv.at[at, z], s_own.at[to, 1], r_in.at[k, 1, j], device),
        ]

    def onward(j, k, to, into, device):
        b, d = piece(j, k)
        return [
            remote(b, b, s_fwd.at[to, 0], r_in.at[into, 0, j], device),
            remote(d, d, s_fwd.at[to, 1], r_in.at[into, 1, j], device),
        ]

    def arrived(j, k):
        for copy in onward(j, k, 0, k, (sn, zm)):
            copy.wait_recv()

    def rhs_piece(j):
        at = pl.ds(j * CHUNK, CHUNK)
        return remote(rl.at[at], rin.at[at], s_rhs, r_rhs.at[j], (other, zo))

    def send_own(j):
        @pl.when(hub)
        def _():
            for copy in own(j, 0, 2, (sn, zm)) + own(j, 1, 0, (other, z)):
                copy.start()

        @pl.when(guest)
        def _():
            rhs_piece(j).start()
            for copy in own(j, 0, 1, (sn, zo)):
                copy.start()

    send_own(0)
    to_guest = remote(st, stv, s_st, r_st, (other, z))

    @pl.when(hub)
    def _():
        to_guest.start()

    def share_rhs(k):
        return remote(rt.at[0, at_cols(k)], rtop.at[c], s_rt.at[k], r_rt.at[c], worker(k))

    def rhs_from(m):
        return remote(rtop.at[m], rtop.at[m], s_rt.at[0], r_rt.at[m], (4 * g + m, zo))

    def not_me(k):
        return jnp.logical_or(guest, place != k)

    def not_own(m):
        return jnp.logical_or(guest, c != m)

    for k in range(4):

        @pl.when(not_me(k))
        def _(k=k):
            share_rhs(k).start()

    for j in range(1, AHEAD):
        send_own(j)

    def top_z(i):
        there = (sn, lax.rem(z + i, 4))
        copies = [remote(td.at[0], tg.at[c, 0, z], s_top.at[i], r_top.at[i], there)]
        for l in range(1, 6):
            copies.append(remote(tb.at[ancestors[l], 0], tg.at[c, l, z], s_top.at[i], r_top.at[i], there))
        return copies

    def top_z_all(i):
        src = lax.rem(z + 4 - i, 4)
        view = tg.at[c, :, src]
        return remote(view, view, s_top.at[i], r_top.at[i], (sn, lax.rem(z + i, 4)))

    for i in range(1, 4):
        for copy in top_z(i):
            copy.start()

    def share_group(i):
        return remote(tg.at[c], tg.at[c], s_grp.at[i], r_grp.at[i], (sibling(i), z))

    def share_upper():
        there = (4 * solver + c, z)
        return [
            remote(tg.at[3, 0], upper.at[g, 0], s_up, r_up.at[g], there),
            remote(tg.at[3, pl.ds(3, 3)], upper.at[g, pl.ds(1, 3)], s_up, r_up.at[g], there),
        ]

    def upper_all(at):
        return remote(upper.at[at], upper.at[at], s_up, r_up.at[at], (4 * solver + c, z))

    for copy in locals_:
        copy.wait()

    @pl.when(hub)
    def _():
        for copy in hub_locals:
            copy.wait()

    @pl.when(guest)
    def _():
        to_guest.wait_recv()

    into_smem = pltpu.make_async_copy(stv, slot_ref, l_sem.at[11])
    into_smem.start()
    into_smem.wait()

    def slot_of(s, r):
        v = slot_ref[s, r]
        t = v - (leaf - 1)
        level = 0
        for l in range(1, 6):
            level = level + jnp.where((t & ((1 << l) - 1)) == 0, 1, 0)
        return jnp.where(v < leaf, v, leaf + level)

    def leaf_block(s):
        return blk[s].reshape(3 * w, w), dinv[s].reshape(w, w)

    def forward_step(s):
        b, d = leaf_block(s)
        solved = dot3(rin[s] + acc[s], d, True)
        fwd[s] = solved
        out = dot3(solved, b, True)
        acc[s + 1] = acc[s + 1] - out[:, :w]
        first, second = slot_of(s, 1), slot_of(s, 2)
        out1, out2 = out[:, w : 2 * w], out[:, 2 * w :]

        def push(t):
            m1 = (first == t).astype(f32)
            m2 = (second == t).astype(f32)
            acc[t] = acc[t] - (m1 * out1 + m2 * out2)

        for t in range(2, leaf + 6):
            push(t)

    def turn(j, carry):
        @pl.when(j + AHEAD < chunks)
        def _():
            send_own(j + AHEAD)

        @pl.when(hub)
        def _():
            @pl.when(j < chunks)
            def _():
                arrived(j, 1)
                for copy in onward(j, 1, 0, 3, (sn, zm)) + onward(j, 1, 1, 1, (other, z)):
                    copy.start()
                arrived(j, 2)
                for copy in onward(j, 2, 2, 2, (other, z)):
                    copy.start()

            @pl.when(j >= 1)
            def _():
                arrived(j - 1, 3)
                for copy in onward(j - 1, 3, 3, 3, (other, z)):
                    copy.start()

        @pl.when(j == min(TOP_Z, chunks))
        def _():
            for i in range(1, 4):
                top_z_all(i).wait_recv()
            for i in range(1, 4):
                share_group(i).start()

        @pl.when(j == min(TOP_GROUP, chunks))
        def _():
            for i in range(1, 4):
                share_group(i).wait_recv()

            @pl.when(jnp.logical_not(is_solver))
            def _():
                for copy in share_upper():
                    copy.start()

        @pl.when(j >= 1)
        def _():
            @pl.when(guest)
            def _():
                rhs_piece(j - 1).wait_recv()
                for k in range(4):
                    arrived(j - 1, k)

            for i in range(CHUNK):
                forward_step((j - 1) * CHUNK + i)

        return carry

    lax.fori_loop(0, chunks + 1, turn, 0)

    def share_part(i):
        to, device = mate(place, i)
        return remote(acc.at[pl.ds(leaf, 6), at_cols(to)], part.at[place], s_part.at[i], r_part.at[i], device)

    for i in range(1, 4):
        share_part(i).start()
    part[place] = acc[pl.ds(leaf, 6), my_cols]

    for m in range(4):

        @pl.when(not_own(m))
        def _(m=m):
            rhs_from(m).wait_recv()

    for i in range(1, 4):
        share_part(i).wait_recv()

    def top_block(m, l):
        return tg[m, l].reshape(w, w)

    def top_stack(m):
        return tg[m, 2:6].reshape(4 * w, w)

    path = part[0] + part[1] + part[2] + part[3]
    f0 = dot3(path[0] + rtop[0], top_block(0, 0), True)
    f1 = dot3(path[1] + rtop[1] - dot3(f0, top_block(0, 1), True), top_block(1, 0), True)
    f2 = dot3(rtop[2], top_block(2, 0), True)
    out = dot3(f0, top_stack(0), True) + dot3(f1, top_stack(1), True) + dot3(f2, top_stack(2), True)
    ftop[0], ftop[1], ftop[2] = f0, f1, f2
    last = 4 * g + 3
    above = [(last + 1) % (1 << l) == 0 for l in range(6)]
    for l in range(2, 6):
        mine = above[l]
        if l < 5:
            mine = jnp.logical_and(mine, jnp.logical_not(above[l + 1]))
        contrib[l - 2] = path[l] + mine.astype(f32) * rtop[3] - out[:, (l - 2) * w : (l - 1) * w]

    def share_contrib():
        return remote(contrib, gathered.at[g], s_con, r_con.at[g], (4 * solver + c, z))

    def contrib_from(at):
        return remote(gathered.at[at], gathered.at[at], s_con, r_con.at[at], (4 * solver + c, z))

    def share_x(i):
        to = lax.rem(g + i, 8)
        return remote(xs.at[to], xpath, s_x.at[i], r_x, (classmate(i), z))

    @pl.when(jnp.logical_not(is_solver))
    def _():
        share_contrib().start()

    @pl.when(is_solver)
    def _():
        upper[g, 0] = tg[3, 0]
        upper[g, 1:4] = tg[3, 3:6]
        gathered[g] = contrib[...]
        for i in range(1, 8):
            at = lax.rem(g + i, 8)
            upper_all(at).wait_recv()
            contrib_from(at).wait_recv()

        def upper_block(q, slot):
            return upper[q, slot].reshape(w, w)

        spans = [range(q + 1 - (1 << trailing(q)), q) for q in range(8)]
        order = sorted(range(8), key=lambda q: (trailing(q), q))
        forward = {}
        for q in order:
            level = trailing(q)
            source = gathered[q, level]
            for below in spans[q]:
                source = source + gathered[below, level]
            for below in spans[q]:
                source = source - dot3(forward[below], upper_block(below, level), True)
            forward[q] = dot3(source, upper_block(q, 0), True)
        solved = {}
        for q in reversed(order):
            source = forward[q]
            for up in range(q + 1, 8):
                if q in spans[up]:
                    source = source - dot3(solved[up], upper_block(q, trailing(up)), False)
            solved[q] = dot3(source, upper_block(q, 0), False)
        for to in range(8):
            for level in range(4):
                q = (to >> level) * (1 << level) + (1 << level) - 1
                if trailing(q) == level:
                    xs[to, level] = solved[q]
                else:
                    xs[to, level] = jnp.zeros((cc, w), f32)
        for i in range(1, 8):
            share_x(i).start()
        xpath[...] = xs[g]

    @pl.when(jnp.logical_not(is_solver))
    def _():
        remote(xpath, xpath, s_x.at[0], r_x, (4 * solver + c, z)).wait_recv()

    across = jnp.concatenate([xpath[0], xpath[1], xpath[2], xpath[3]], axis=1)
    x1 = dot3(ftop[1] - dot3(across, top_stack(1), False), top_block(1, 0), False)
    x2 = dot3(ftop[2] - dot3(across, top_stack(2), False), top_block(2, 0), False)
    x0 = dot3(
        ftop[0] - dot3(across, top_stack(0), False) - dot3(x1, top_block(0, 1), False), top_block(0, 0), False
    )
    zown[0], zown[1], zown[6] = x0, x1, x2
    zown[2:6] = xpath[...]

    def share_z(i):
        to, device = mate(place, i)
        return remote(zown.at[pl.ds(0, 6)], zbuf.at[pl.ds(leaf, 6), my_cols], s_z.at[i], r_z.at[i], device)

    def z_from(i):
        view = zbuf.at[pl.ds(leaf, 6), at_cols(lax.rem(place + 4 - i, 4))]
        return remote(zown.at[pl.ds(0, 6)], view, s_z.at[i], r_z.at[i], mate(place, i)[1])

    for i in range(1, 4):
        share_z(i).start()
    zbuf[pl.ds(leaf, 6), my_cols] = zown[0:6]

    def level_of(t):
        return sum(jnp.where((t + 1) % (1 << l) == 0, 1, 0) for l in range(1, 6))

    top_slots = (0, 1, 6, level_of(last))

    def share_top(m):
        return remote(zown.at[top_slots[m]], tout.at[my_cols], s_to.at[m], r_to.at[place], (4 * g + m, block))

    def top_from(k):
        return remote(zown.at[0], tout.at[at_cols(k)], s_to.at[0], r_to.at[k], worker(k))

    for m in range(4):

        @pl.when(not_own(m))
        def _(m=m):
            share_top(m).start()

    @pl.when(hub)
    def _():
        tout[my_cols] = zown[jnp.where(c == 2, 6, level_of(sn))]

    for i in range(1, 4):
        z_from(i).wait_recv()

    def back_piece(j):
        at = pl.ds(leaf - (j + 1) * CHUNK, CHUNK)
        return remote(zbuf.at[at], o_leaf.at[at], s_back, r_back, (other, zo))

    def keep_piece(j):
        at = pl.ds(leaf - (j + 1) * CHUNK, CHUNK)
        return pltpu.make_async_copy(zbuf.at[at], o_leaf.at[at], l_sem.at[0])

    def let_go(j):
        @pl.when(hub)
        def _():
            keep_piece(j).start()

        @pl.when(guest)
        def _():
            back_piece(j).start()

    def backward(j, carry):
        for i in range(CHUNK):
            s = leaf - 1 - j * CHUNK - i
            b, d = leaf_block(s)
            z_at = jnp.concatenate([zbuf[s + 1], zbuf[slot_of(s, 1)], zbuf[slot_of(s, 2)]], axis=1)
            zbuf[s] = dot3(fwd[s] - dot3(z_at, b, False), d, False)

        @pl.when(j >= 1)
        def _():
            let_go(j - 1)

        return carry

    lax.fori_loop(0, chunks, backward, 0)

    for k in range(4):

        @pl.when(not_me(k))
        def _(k=k):
            top_from(k).wait_recv()

    top_out = pltpu.make_async_copy(tout, o_top.at[0], l_sem.at[1])
    top_out.start()
    let_go(chunks - 1)

    whole = pl.ds(0, leaf)

    def left(ssem, rows):
        b, d = blk.at[:, :, rows], dinv.at[:, rows]
        remote(b, b, ssem.at[0], r_in.at[0, 0, 0], (sn, zo)).wait_send()
        remote(d, d, ssem.at[1], r_in.at[0, 1, 0], (sn, zo)).wait_send()

    left(s_own.at[0], z)
    for i in range(1, 4):
        top_z_all(i).wait_send()
        share_group(i).wait_send()
        share_part(i).wait_send()
        share_z(i).wait_send()
    for m in range(4):

        @pl.when(not_me(m))
        def _(m=m):
            share_rhs(m).wait_send()

        @pl.when(not_own(m))
        def _(m=m):
            share_top(m).wait_send()

    @pl.when(jnp.logical_not(is_solver))
    def _():
        upper_all(g).wait_send()
        share_contrib().wait_send()

    @pl.when(is_solver)
    def _():
        for i in range(1, 8):
            share_x(i).wait_send()

    @pl.when(hub)
    def _():
        left(s_own.at[1], z)
        for to in range(4):
            left(s_fwd.at[to], z)
        to_guest.wait_send()
        pltpu.make_async_copy(zbuf.at[whole], o_leaf, l_sem.at[0]).wait()

    @pl.when(guest)
    def _():
        remote(rl, rin, s_rhs, r_rhs.at[0], (other, zo)).wait_send()
        everything = remote(zbuf.at[whole], o_leaf, s_back, r_back, (other, zo))
        everything.wait_send()
        everything.wait_recv()

    top_out.wait()


def local(rl, rt, lb, ld, st, tb, td):
    leaf, cols, w = rl.shape
    cc, quarter, chunks = cols // 4, w // 4, leaf // CHUNK
    any_spec = pl.BlockSpec(memory_space=pl.ANY)
    dma = pltpu.SemaphoreType.DMA
    return pl.pallas_call(
        kernel,
        out_shape=(jax.ShapeDtypeStruct(rl.shape, f32), jax.ShapeDtypeStruct(rt.shape, f32)),
        in_specs=[any_spec] * 7,
        out_specs=(any_spec, any_spec),
        scratch_shapes=[
            pltpu.VMEM((leaf + 6, cols, w), f32),
            pltpu.VMEM((leaf, cols, w), f32),
            pltpu.VMEM((leaf, 3, 4, quarter, w), f32),
            pltpu.VMEM((leaf, 4, quarter, w), f32),
            pltpu.VMEM((leaf, cols, w), f32),
            pltpu.VMEM((leaf + 6, cols, w), f32),
            pltpu.VMEM((4, 6, 4, quarter, w), f32),
            pltpu.VMEM((4, cc, w), f32),
            pltpu.VMEM((4, 6, cc, w), f32),
            pltpu.VMEM((4, cc, w), f32),
            pltpu.VMEM((8, 4, cc, w), f32),
            pltpu.VMEM((8, 4, 4, quarter, w), f32),
            pltpu.VMEM((8, 4, cc, w), f32),
            pltpu.VMEM((4, cc, w), f32),
            pltpu.VMEM((7, cc, w), f32),
            pltpu.VMEM((3, cc, w), f32),
            pltpu.VMEM((cols, w), f32),
            pltpu.VMEM(st.shape, jnp.int32),
            pltpu.SMEM(st.shape, jnp.int32),
            dma((2, 2)), dma((4, 2)), dma, dma, dma((4, 2, chunks)), dma((chunks,)), dma,
            dma((4,)), dma((4,)), dma((4,)), dma((4,)), dma((4,)), dma((4,)),
            dma, dma((8,)), dma((4,)), dma((4,)), dma, dma((8,)), dma((8,)), dma, dma((4,)), dma((4,)),
            dma((4,)), dma((4,)), dma, dma, dma((12,)),
        ],
        compiler_params=pltpu.CompilerParams(
            collective_id=0, has_side_effects=True, vmem_limit_bytes=60 * 1024 * 1024
        ),
        name="substitution",
    )(st, rl, rt, lb, ld, tb, td)


def solution(mesh):
    return jax.shard_map(
        local,
        mesh=mesh,
        in_specs=(
            P("sn", "rhs", None),
            P("sn", "rhs", None),
            P("sn", None, "rhs", None),
            P("sn", "rhs", None),
            P("sn", None),
            P(None, "sn", "rhs", None),
            P("sn", "rhs", None),
        ),
        out_specs=(P("sn", "rhs", None), P("sn", "rhs", None)),
        check_vma=False,
    )
```

time: 132 us -> 129 us (0.977)
  other arithmetic: 1.33 us -> 0 us
    pallas_call x1, Pallas kernels: 125 us -> 124 us  [local(): pl.pallas_call(kernel, out_shape=(jax.ShapeDtypeStruct(rl.shape, f32), ja...]
where the time goes in v2:
time: 129 us
  Pallas kernels  124 us (96%)
  local copies, waits for them, and re-layouts  4.3 us (3%)
    pallas_call x1, Pallas kernels, local(): pl.pallas_call(kernel, out_shape=(jax.ShapeDtypeStruct(rl.shape, f32), ja...  124 us
    unnamed x5, local copies, waits for them, and re-layouts  4.3 us

profile of v2, /device:TPU:1, one launch (start us, length us, event | category | flops | bytes accessed | tf_op | source)
XLA Modules:
  0.0 129.1 jit_solution(12944584258638246033)
XLA Ops:
  0.6 1.4 %copy.9.st = s32[32,3]{1,0:T(8,128)} copy(s32[32,3]{0,1:T(4,128)} %param.11) | data formatting | bytes 768 | tf_op args[4]
  2.0 124.1 %substitution.1 = (f32[32,64,128]{2,1,0:T(8,128)}, f32[1,64,128]{2,1,0:T(8,128)}) custom-call(s32[32,3]{1,0:T(8,128)} %copy.9.st, f32[32,64,128]{2,1,0:T(8,128)} %rl.1, f32[1,64,128]{2,1,0:T(8,128)} %rt.1, f32[32,3,32,128]{3,2,1,0:T(8,128)} %lb.1, f32[32,32,128]{2,1,0:T(8,128)} %ld.1, f32[32,1,32,128]{3,2,1,0:T(8,128)} %tb.1, f32[1,32,128]{2,1,0:T(8,128)} %td.1), custom_call_target="tpu_custom_call" | custom-call | tf_op jit(solution)/shard_map/substitution/pallas_call | solution.py:560
  126.1 0.0 copy-start
  126.1 2.3 %copy.12 = f32[32,64,128]{2,1,0:T(8,128)} copy(f32[32,64,128]{2,1,0:T(8,128)} %get-tuple-element.4) | data formatting | bytes 2097152
  128.4 0.0 copy-done
  128.4 0.6 copy.13
Async XLA Ops:
  126.1 2.3 %copy-start = (f32[1,64,128]{2,1,0:T(8,128)S(1)}, f32[1,64,128]{2,1,0:T(8,128)}, u32[]{:S(2)}) copy-start(f32[1,64,128]{2,1,0:T(8,128)} %get-tuple-element.5) | copy-start | bytes 98308

commit v3 on v2

--- a/solution.py
+++ b/solution.py
@@ -12,8 +12,9 @@
 bf16 = jnp.bfloat16
 
 CHUNK = 2
-AHEAD = 2
-TOP_Z, TOP_GROUP, TOP_SOLVER = 3, 6, 10
+AHEAD = 3
+LAG = 2
+TOP_Z, TOP_GROUP = 3, 11
 
 
 def split(x):
@@ -187,7 +188,7 @@
         def _(k=k):
             share_rhs(k).start()
 
-    for j in range(1, AHEAD):
+    for j in range(1, min(AHEAD, chunks)):
         send_own(j)
 
     def top_z(i):
@@ -279,10 +280,10 @@
                 for copy in onward(j, 2, 2, 2, (other, z)):
                     copy.start()
 
-            @pl.when(j >= 1)
+            @pl.when(j >= LAG)
             def _():
-                arrived(j - 1, 3)
-                for copy in onward(j - 1, 3, 3, 3, (other, z)):
+                arrived(j - LAG, 3)
+                for copy in onward(j - LAG, 3, 3, 3, (other, z)):
                     copy.start()
 
         @pl.when(j == min(TOP_Z, chunks))
@@ -302,20 +303,20 @@
                 for copy in share_upper():
                     copy.start()
 
-        @pl.when(j >= 1)
+        @pl.when(j >= LAG)
         def _():
             @pl.when(guest)
             def _():
-                rhs_piece(j - 1).wait_recv()
+                rhs_piece(j - LAG).wait_recv()
                 for k in range(4):
-                    arrived(j - 1, k)
+                    arrived(j - LAG, k)
 
             for i in range(CHUNK):
-                forward_step((j - 1) * CHUNK + i)
+                forward_step((j - LAG) * CHUNK + i)
 
         return carry
 
-    lax.fori_loop(0, chunks + 1, turn, 0)
+    lax.fori_loop(0, chunks + LAG, turn, 0)
 
     def share_part(i):
         to, device = mate(place, i)

time: 129 us -> 107 us (0.83)
  Pallas kernels: 124 us -> 102 us
    pallas_call x1, Pallas kernels: 124 us -> 102 us  [local(): pl.pallas_call(kernel, out_shape=(jax.ShapeDtypeStruct(rl.shape, f32), ja...]
where the time goes in v3:
time: 107 us
  Pallas kernels  102 us (95%)
  local copies, waits for them, and re-layouts  4.3 us (4%)
    pallas_call x1, Pallas kernels, local(): pl.pallas_call(kernel, out_shape=(jax.ShapeDtypeStruct(rl.shape, f32), ja...  102 us
    unnamed x5, local copies, waits for them, and re-layouts  4.3 us

profile of v3, /device:TPU:1, one launch (start us, length us, event | category | flops | bytes accessed | tf_op | source)
XLA Modules:
  0.0 107.3 jit_solution(6481973057713991672)
XLA Ops:
  0.6 1.4 %copy.9.st = s32[32,3]{1,0:T(8,128)} copy(s32[32,3]{0,1:T(4,128)} %param.11) | data formatting | bytes 768 | tf_op args[4]
  2.0 102.4 %substitution.1 = (f32[32,64,128]{2,1,0:T(8,128)}, f32[1,64,128]{2,1,0:T(8,128)}) custom-call(s32[32,3]{1,0:T(8,128)} %copy.9.st, f32[32,64,128]{2,1,0:T(8,128)} %rl.1, f32[1,64,128]{2,1,0:T(8,128)} %rt.1, f32[32,3,32,128]{3,2,1,0:T(8,128)} %lb.1, f32[32,32,128]{2,1,0:T(8,128)} %ld.1, f32[32,1,32,128]{3,2,1,0:T(8,128)} %tb.1, f32[1,32,128]{2,1,0:T(8,128)} %td.1), custom_call_target="tpu_custom_call" | custom-call | tf_op jit(solution)/shard_map/substitution/pallas_call | solution.py:561
  104.4 0.0 copy-start
  104.4 2.3 %copy.12 = f32[32,64,128]{2,1,0:T(8,128)} copy(f32[32,64,128]{2,1,0:T(8,128)} %get-tuple-element.4) | data formatting | bytes 2097152
  106.7 0.0 copy-done
  106.7 0.6 copy.13
Async XLA Ops:
  104.4 2.3 %copy-start = (f32[1,64,128]{2,1,0:T(8,128)S(1)}, f32[1,64,128]{2,1,0:T(8,128)}, u32[]{:S(2)}) copy-start(f32[1,64,128]{2,1,0:T(8,128)} %get-tuple-element.5) | copy-start | bytes 98308

commit v4 on v3

--- a/solution.py
+++ b/solution.py
@@ -14,7 +14,7 @@
 CHUNK = 2
 AHEAD = 3
 LAG = 2
-TOP_Z, TOP_GROUP = 3, 11
+TOP_TURNS = 1, 3, 7, 8
 
 
 def split(x):
@@ -42,7 +42,7 @@
     o_leaf, o_top,
     acc, rin, blk, dinv, fwd, zbuf, tg, rtop, part, contrib, gathered, upper, xs, xpath, zown, ftop, tout, stv, slot_ref,
     s_own, s_fwd, s_rhs, s_back, r_in, r_rhs, r_back,
-    s_top, r_top, s_rt, r_rt, s_grp, r_grp, s_up, r_up, s_part, r_part, s_con, r_con, s_x, r_x, s_z, r_z, s_to, r_to,
+    s_top, r_top, s_rt, r_rt, s_grp, r_grp, s_up, r_up, s_part, r_part, s_con, r_con, s_z, r_z, s_to, r_to,
     s_st, r_st, l_sem,
 ):
     leaf, cols, w = rl.shape
@@ -58,8 +58,6 @@
     other, zm, zo = sn + 1 - 2 * core, z + 1 - 2 * (z % 2), 3 - z
     rows_of = (z, zo, zm, 3 - zm)
     place = 2 * (c // 2) + role
-    solver = 2 * c
-    is_solver = g == solver
     block = jnp.where(hub, z, zo)
 
     def at_cols(k):
@@ -164,61 +162,69 @@
                 copy.start()
 
     send_own(0)
-    to_guest = remote(st, stv, s_st, r_st, (other, z))
-
-    @pl.when(hub)
-    def _():
-        to_guest.start()
-
-    def share_rhs(k):
-        return remote(rt.at[0, at_cols(k)], rtop.at[c], s_rt.at[k], r_rt.at[c], worker(k))
-
-    def rhs_from(m):
-        return remote(rtop.at[m], rtop.at[m], s_rt.at[0], r_rt.at[m], (4 * g + m, zo))
-
-    def not_me(k):
-        return jnp.logical_or(guest, place != k)
-
-    def not_own(m):
-        return jnp.logical_or(guest, c != m)
-
-    for k in range(4):
-
-        @pl.when(not_me(k))
-        def _(k=k):
-            share_rhs(k).start()
-
-    for j in range(1, min(AHEAD, chunks)):
-        send_own(j)
 
     def top_z(i):
-        there = (sn, lax.rem(z + i, 4))
+        there = (sn, (zm, zo)[i])
         copies = [remote(td.at[0], tg.at[c, 0, z], s_top.at[i], r_top.at[i], there)]
         for l in range(1, 6):
             copies.append(remote(tb.at[ancestors[l], 0], tg.at[c, l, z], s_top.at[i], r_top.at[i], there))
         return copies
 
     def top_z_all(i):
-        src = lax.rem(z + 4 - i, 4)
-        view = tg.at[c, :, src]
-        return remote(view, view, s_top.at[i], r_top.at[i], (sn, lax.rem(z + i, 4)))
-
-    for i in range(1, 4):
+        view = tg.at[c, :, (zm, zo, zm)[i]]
+        return remote(view, view, s_top.at[i], r_top.at[i], (sn, (zm, zo, zo)[i]))
+
+    for i in range(2):
         for copy in top_z(i):
             copy.start()
 
+    to_guest = remote(st, stv, s_st, r_st, (other, z))
+
+    @pl.when(hub)
+    def _():
+        to_guest.start()
+
+    def share_rhs(k):
+        return remote(rt.at[0, at_cols(k)], rtop.at[c], s_rt.at[k], r_rt.at[c], worker(k))
+
+    def rhs_from(m):
+        return remote(rtop.at[m], rtop.at[m], s_rt.at[0], r_rt.at[m], (4 * g + m, zo))
+
+    def not_me(k):
+        return jnp.logical_or(guest, place != k)
+
+    def not_own(m):
+        return jnp.logical_or(guest, c != m)
+
+    for k in range(4):
+
+        @pl.when(not_me(k))
+        def _(k=k):
+            share_rhs(k).start()
+
+    for j in range(1, min(AHEAD, chunks)):
+        send_own(j)
+
     def share_group(i):
-        return remote(tg.at[c], tg.at[c], s_grp.at[i], r_grp.at[i], (sibling(i), z))
-
-    def share_upper():
-        there = (4 * solver + c, z)
-        return [
-            remote(tg.at[3, 0], upper.at[g, 0], s_up, r_up.at[g], there),
-            remote(tg.at[3, pl.ds(3, 3)], upper.at[g, pl.ds(1, 3)], s_up, r_up.at[g], there),
-        ]
-
-    def upper_all(at):
-        return remote(upper.at[at], upper.at[at], s_up, r_up.at[at], (4 * solver + c, z))
+        what = (c, c, lax.rem(c + 2, 4))[i]
+        there = (4 * g + lax.rem(c + 2, 4), other, other)[i]
+        return remote(tg.at[what], tg.at[what], s_grp.at[i], r_grp.at[i], (there, z))
+
+    def exists(q, level):
+        return (q // (1 << level)) % 2 == 0
+
+    def share_upper(i, slot):
+        return remote(
+            tg.at[3, slot if slot == 0 else slot + 2], upper.at[g, slot], s_up.at[i, slot], r_up.at[g, slot],
+            (classmate(i), z),
+        )
+
+    def upper_from(at, slot):
+        view = upper.at[at, slot]
+        return remote(view, view, s_up.at[0, slot], r_up.at[at, slot], (4 * at + c, z))
+
+    def has_upper(q, slot):
+        return jnp.logical_and(exists(q, slot), (q + 1) % (1 << slot) != 0)
 
     for copy in locals_:
         copy.wait()
@@ -237,7 +243,7 @@
     into_smem.wait()
 
     def slot_of(s, r):
-        v = slot_ref[s, r]
+        v = slot_ref[r, s]
         t = v - (leaf - 1)
         level = 0
         for l in range(1, 6):
@@ -286,22 +292,35 @@
                 for copy in onward(j - LAG, 3, 3, 3, (other, z)):
                     copy.start()
 
-        @pl.when(j == min(TOP_Z, chunks))
-        def _():
-            for i in range(1, 4):
-                top_z_all(i).wait_recv()
-            for i in range(1, 4):
+        @pl.when(j == TOP_TURNS[0])
+        def _():
+            top_z_all(0).wait_recv()
+            top_z_all(2).start()
+
+        @pl.when(j == TOP_TURNS[1])
+        def _():
+            top_z_all(1).wait_recv()
+            top_z_all(2).wait_recv()
+            for i in range(2):
                 share_group(i).start()
 
-        @pl.when(j == min(TOP_GROUP, chunks))
-        def _():
-            for i in range(1, 4):
-                share_group(i).wait_recv()
-
-            @pl.when(jnp.logical_not(is_solver))
-            def _():
-                for copy in share_upper():
-                    copy.start()
+        @pl.when(j == TOP_TURNS[2])
+        def _():
+            share_group(0).wait_recv()
+            share_group(2).start()
+
+        @pl.when(j == TOP_TURNS[3])
+        def _():
+            share_group(1).wait_recv()
+            share_group(2).wait_recv()
+            for i in range(1, 8):
+                share_upper(i, 0).start()
+            for slot in range(1, 4):
+
+                @pl.when(has_upper(g, slot))
+                def _(slot=slot):
+                    for i in range(1, 8):
+                        share_upper(i, slot).start()
 
         @pl.when(j >= LAG)
         def _():
@@ -355,65 +374,67 @@
             mine = jnp.logical_and(mine, jnp.logical_not(above[l + 1]))
         contrib[l - 2] = path[l] + mine.astype(f32) * rtop[3] - out[:, (l - 2) * w : (l - 1) * w]
 
-    def share_contrib():
-        return remote(contrib, gathered.at[g], s_con, r_con.at[g], (4 * solver + c, z))
-
-    def contrib_from(at):
-        return remote(gathered.at[at], gathered.at[at], s_con, r_con.at[at], (4 * solver + c, z))
-
-    def share_x(i):
-        to = lax.rem(g + i, 8)
-        return remote(xs.at[to], xpath, s_x.at[i], r_x, (classmate(i), z))
-
-    @pl.when(jnp.logical_not(is_solver))
-    def _():
-        share_contrib().start()
-
-    @pl.when(is_solver)
-    def _():
-        upper[g, 0] = tg[3, 0]
-        upper[g, 1:4] = tg[3, 3:6]
-        gathered[g] = contrib[...]
-        for i in range(1, 8):
-            at = lax.rem(g + i, 8)
-            upper_all(at).wait_recv()
-            contrib_from(at).wait_recv()
-
-        def upper_block(q, slot):
-            return upper[q, slot].reshape(w, w)
-
-        spans = [range(q + 1 - (1 << trailing(q)), q) for q in range(8)]
-        order = sorted(range(8), key=lambda q: (trailing(q), q))
-        forward = {}
-        for q in order:
-            level = trailing(q)
-            source = gathered[q, level]
-            for below in spans[q]:
-                source = source + gathered[below, level]
-            for below in spans[q]:
-                source = source - dot3(forward[below], upper_block(below, level), True)
-            forward[q] = dot3(source, upper_block(q, 0), True)
-        solved = {}
-        for q in reversed(order):
-            source = forward[q]
-            for up in range(q + 1, 8):
-                if q in spans[up]:
-                    source = source - dot3(solved[up], upper_block(q, trailing(up)), False)
-            solved[q] = dot3(source, upper_block(q, 0), False)
-        for to in range(8):
-            for level in range(4):
-                q = (to >> level) * (1 << level) + (1 << level) - 1
-                if trailing(q) == level:
-                    xs[to, level] = solved[q]
-                else:
-                    xs[to, level] = jnp.zeros((cc, w), f32)
-        for i in range(1, 8):
-            share_x(i).start()
-        xpath[...] = xs[g]
-
-    @pl.when(jnp.logical_not(is_solver))
-    def _():
-        remote(xpath, xpath, s_x.at[0], r_x, (4 * solver + c, z)).wait_recv()
+    def share_contrib(i, level):
+        return remote(
+            contrib.at[level], gathered.at[g, level], s_con.at[i, level], r_con.at[g, level], (classmate(i), z)
+        )
+
+    def contrib_from(at, level):
+        view = gathered.at[at, level]
+        return remote(view, view, s_con.at[0, level], r_con.at[at, level], (4 * at + c, z))
+
+    for level in range(4):
+
+        @pl.when(exists(g, level))
+        def _(level=level):
+            for i in (4, 3, 5, 2, 6, 1, 7):
+                share_contrib(i, level).start()
+
+    upper[g, 0] = tg[3, 0]
+    upper[g, 1:4] = tg[3, 3:6]
+    gathered[g] = contrib[...]
+    for i in range(1, 8):
+        at = lax.rem(g + i, 8)
+        upper_from(at, 0).wait_recv()
+        for slot in range(1, 4):
+
+            @pl.when(has_upper(at, slot))
+            def _(at=at, slot=slot):
+                upper_from(at, slot).wait_recv()
+
+    for i in range(1, 8):
+        at = lax.rem(g + i, 8)
+        for level in range(4):
+
+            @pl.when(exists(at, level))
+            def _(at=at, level=level):
+                contrib_from(at, level).wait_recv()
+
+    def upper_block(q, slot):
+        return upper[q, slot].reshape(w, w)
+
+    spans = [range(q + 1 - (1 << trailing(q)), q) for q in range(8)]
+    order = sorted(range(8), key=lambda q: (trailing(q), q))
+    forward = {}
+    for q in order:
+        level = trailing(q)
+        source = gathered[q, level]
+        for below in spans[q]:
+            source = source + gathered[below, level]
+        for below in spans[q]:
+            source = source - dot3(forward[below], upper_block(below, level), True)
+        forward[q] = dot3(source, upper_block(q, 0), True)
+    solved = {}
+    for q in reversed(order):
+        source = forward[q]
+        for up in range(q + 1, 8):
+            if q in spans[up]:
+                source = source - dot3(solved[up], upper_block(q, trailing(up)), False)
+        solved[q] = dot3(source, upper_block(q, 0), False)
+        xs[q] = solved[q]
+    for level in range(4):
+        q = (g // (1 << level)) * (1 << level) + (1 << level) - 1
+        xpath[level] = xs[q] * exists(g, level).astype(f32)
 
     across = jnp.concatenate([xpath[0], xpath[1], xpath[2], xpath[3]], axis=1)
     x1 = dot3(ftop[1] - dot3(across, top_stack(1), False), top_block(1, 0), False)
@@ -510,11 +531,11 @@
         remote(d, d, ssem.at[1], r_in.at[0, 1, 0], (sn, zo)).wait_send()
 
     left(s_own.at[0], z)
-    for i in range(1, 4):
+    for i in range(3):
         top_z_all(i).wait_send()
         share_group(i).wait_send()
-        share_part(i).wait_send()
-        share_z(i).wait_send()
+        share_part(i + 1).wait_send()
+        share_z(i + 1).wait_send()
     for m in range(4):
 
         @pl.when(not_me(m))
@@ -525,15 +546,21 @@
         def _(m=m):
             share_top(m).wait_send()
 
-    @pl.when(jnp.logical_not(is_solver))
-    def _():
-        upper_all(g).wait_send()
-        share_contrib().wait_send()
-
-    @pl.when(is_solver)
-    def _():
-        for i in range(1, 8):
-            share_x(i).wait_send()
+    for i in range(1, 8):
+        share_upper(i, 0).wait_send()
+    for slot in range(1, 4):
+
+        @pl.when(has_upper(g, slot))
+        def _(slot=slot):
+            for i in range(1, 8):
+                share_upper(i, slot).wait_send()
+
+    for level in range(4):
+
+        @pl.when(exists(g, level))
+        def _(level=level):
+            for i in range(1, 8):
+                share_contrib(i, level).wait_send()
 
     @pl.when(hub)
     def _():
@@ -557,12 +584,13 @@
     leaf, cols, w = rl.shape
     cc, quarter, chunks = cols // 4, w // 4, leaf // CHUNK
     any_spec = pl.BlockSpec(memory_space=pl.ANY)
+    operands = [pltpu.with_memory_space_constraint(v, pltpu.HBM) for v in (st.T, rl, rt, lb, ld, tb, td)]
     dma = pltpu.SemaphoreType.DMA
     return pl.pallas_call(
         kernel,
         out_shape=(jax.ShapeDtypeStruct(rl.shape, f32), jax.ShapeDtypeStruct(rt.shape, f32)),
         in_specs=[any_spec] * 7,
-        out_specs=(any_spec, any_spec),
+        out_specs=(pl.BlockSpec(memory_space=pltpu.VMEM),) * 2,
         scratch_shapes=[
             pltpu.VMEM((leaf + 6, cols, w), f32),
             pltpu.VMEM((leaf, cols, w), f32),
@@ -576,23 +604,23 @@
             pltpu.VMEM((4, cc, w), f32),
             pltpu.VMEM((8, 4, cc, w), f32),
             pltpu.VMEM((8, 4, 4, quarter, w), f32),
-            pltpu.VMEM((8, 4, cc, w), f32),
+            pltpu.VMEM((8, cc, w), f32),
             pltpu.VMEM((4, cc, w), f32),
             pltpu.VMEM((7, cc, w), f32),
             pltpu.VMEM((3, cc, w), f32),
             pltpu.VMEM((cols, w), f32),
-            pltpu.VMEM(st.shape, jnp.int32),
-            pltpu.SMEM(st.shape, jnp.int32),
+            pltpu.VMEM(st.shape[::-1], jnp.int32),
+            pltpu.SMEM(st.shape[::-1], jnp.int32),
             dma((2, 2)), dma((4, 2)), dma, dma, dma((4, 2, chunks)), dma((chunks,)), dma,
             dma((4,)), dma((4,)), dma((4,)), dma((4,)), dma((4,)), dma((4,)),
-            dma, dma((8,)), dma((4,)), dma((4,)), dma, dma((8,)), dma((8,)), dma, dma((4,)), dma((4,)),
+            dma((8, 4)), dma((8, 4)), dma((4,)), dma((4,)), dma((8, 4)), dma((8, 4)), dma((4,)), dma((4,)),
             dma((4,)), dma((4,)), dma, dma, dma((12,)),
         ],
         compiler_params=pltpu.CompilerParams(
-            collective_id=0, has_side_effects=True, vmem_limit_bytes=60 * 1024 * 1024
+            collective_id=0, has_side_effects=True, vmem_limit_bytes=24*1024*1024
         ),
         name="substitution",
-    )(st, rl, rt, lb, ld, tb, td)
+    )(*operands)
 
 
 def solution(mesh):

time: 107 us -> 102 us (0.953)
  local copies, waits for them, and re-layouts: 4.3 us -> 1.59 us
  Pallas kernels: 102 us -> 99.8 us
    unnamed x5 -> x2, local copies, waits for them, and re-layouts: 4.3 us -> 1.59 us
    pallas_call x1, Pallas kernels: 102 us -> 99.8 us  [local(): pl.pallas_call(kernel, out_shape=(jax.ShapeDtypeStruct(rl.shape, f32), ja...]
where the time goes in v4:
time: 102 us
  Pallas kernels  99.8 us (98%)
  local copies, waits for them, and re-layouts  1.59 us (2%)
    pallas_call x1, Pallas kernels, local(): pl.pallas_call(kernel, out_shape=(jax.ShapeDtypeStruct(rl.shape, f32), ja...  99.8 us

profile of v4, /device:TPU:1, one launch (start us, length us, event | category | flops | bytes accessed | tf_op | source)
XLA Modules:
  0.0 102.0 jit_solution(15650798143965247597)
XLA Ops:
  0.6 99.8 %substitution.1 = (f32[32,64,128]{2,1,0:T(8,128)S(1)}, f32[1,64,128]{2,1,0:T(8,128)S(1)}) custom-call(s32[3,32]{1,0:T(4,128)} %bitcast.1, f32[32,64,128]{2,1,0:T(8,128)} %rl.1, f32[1,64,128]{2,1,0:T(8,128)} %rt.1, f32[32,3,32,128]{3,2,1,0:T(8,128)} %lb.1, f32[32,32,128]{2,1,0:T(8,128)} %ld.1, f32[32,1,32,128]{3,2,1,0:T(8,128)} %tb.1, f32[1,32,128]{2,1,0:T(8,128)} %td.1), custom_call_target="tpu_custom_call" | custom-call | tf_op jit(solution)/shard_map/substitution/pallas_call | solution.py:589
  100.4 1.0 copy.11
  101.4 0.6 copy.12

commit v5 on v4

--- a/solution.py
+++ b/solution.py
@@ -13,8 +13,8 @@
 
 CHUNK = 2
 AHEAD = 3
-LAG = 2
-TOP_TURNS = 1, 3, 7, 8
+LAG = 3
+TOP_TURNS = 2, 4, 5, 9, 10
 
 
 def split(x):
@@ -27,7 +27,9 @@
     dot = functools.partial(lax.dot_general, dimension_numbers=dims, preferred_element_type=f32)
     x_high, x_low = split(x)
     w_high, w_low = split(w)
-    return dot(x_high, w_high) + (dot(x_high, w_low) + dot(x_low, w_high))
+    m = x.shape[0]
+    both = dot(jnp.concatenate([x_high, x_low], axis=0), w_high)
+    return both[:m] + (both[m:] + dot(x_high, w_low))
 
 
 def trailing(q):
@@ -300,16 +302,21 @@
         @pl.when(j == TOP_TURNS[1])
         def _():
             top_z_all(1).wait_recv()
-            top_z_all(2).wait_recv()
+            top_z_all(2).wait()
+            column = dot3(tg[c, 1:6].reshape(5 * w, w), tg[c, 0].reshape(w, w), False)
+            tg[c, 1:6] = column.reshape(5, 4, quarter, w)
+
+        @pl.when(j == TOP_TURNS[2])
+        def _():
             for i in range(2):
                 share_group(i).start()
 
-        @pl.when(j == TOP_TURNS[2])
+        @pl.when(j == TOP_TURNS[3])
         def _():
             share_group(0).wait_recv()
             share_group(2).start()
 
-        @pl.when(j == TOP_TURNS[3])
+        @pl.when(j == TOP_TURNS[4])
         def _():
             share_group(1).wait_recv()
             share_group(2).wait_recv()
@@ -351,21 +358,26 @@
         def _(m=m):
             rhs_from(m).wait_recv()
 
+    def top_block(m, l):
+        return tg[m, l].reshape(w, w)
+
+    def top_stack(m, first=2):
+        return tg[m, first:6].reshape((6 - first) * w, w)
+
+    def squared(x, d):
+        return dot3(dot3(x, d, True), d, False)
+
+    source2 = rtop[2]
+    out2 = dot3(source2, top_stack(2), True)
+    upper[g, 0] = tg[3, 0]
+    upper[g, 1:4] = tg[3, 3:6]
     for i in range(1, 4):
         share_part(i).wait_recv()
-
-    def top_block(m, l):
-        return tg[m, l].reshape(w, w)
-
-    def top_stack(m):
-        return tg[m, 2:6].reshape(4 * w, w)
-
     path = part[0] + part[1] + part[2] + part[3]
-    f0 = dot3(path[0] + rtop[0], top_block(0, 0), True)
-    f1 = dot3(path[1] + rtop[1] - dot3(f0, top_block(0, 1), True), top_block(1, 0), True)
-    f2 = dot3(rtop[2], top_block(2, 0), True)
-    out = dot3(f0, top_stack(0), True) + dot3(f1, top_stack(1), True) + dot3(f2, top_stack(2), True)
-    ftop[0], ftop[1], ftop[2] = f0, f1, f2
+    source0 = path[0] + rtop[0]
+    out0 = dot3(source0, top_stack(0, 1), True)
+    source1 = path[1] + rtop[1] - out0[:, :w]
+    out = out0[:, w:] + dot3(source1, top_stack(1), True) + out2
     last = 4 * g + 3
     above = [(last + 1) % (1 << l) == 0 for l in range(6)]
     for l in range(2, 6):
@@ -390,9 +402,10 @@
             for i in (4, 3, 5, 2, 6, 1, 7):
                 share_contrib(i, level).start()
 
-    upper[g, 0] = tg[3, 0]
-    upper[g, 1:4] = tg[3, 3:6]
     gathered[g] = contrib[...]
+    ftop[0] = squared(source0, top_block(0, 0))
+    ftop[1] = squared(source1, top_block(1, 0))
+    ftop[2] = squared(source2, top_block(2, 0))
     for i in range(1, 8):
         at = lax.rem(g + i, 8)
         upper_from(at, 0).wait_recv()
@@ -415,33 +428,31 @@
 
     spans = [range(q + 1 - (1 << trailing(q)), q) for q in range(8)]
     order = sorted(range(8), key=lambda q: (trailing(q), q))
-    forward = {}
+    sources, parts = {}, {}
     for q in order:
         level = trailing(q)
         source = gathered[q, level]
         for below in spans[q]:
             source = source + gathered[below, level]
         for below in spans[q]:
-            source = source - dot3(forward[below], upper_block(below, level), True)
-        forward[q] = dot3(source, upper_block(q, 0), True)
+            source = source - dot3(sources[below], upper_block(below, level), True)
+        sources[q] = source
+        parts[q] = squared(source, upper_block(q, 0))
     solved = {}
     for q in reversed(order):
-        source = forward[q]
+        solved[q] = parts[q]
         for up in range(q + 1, 8):
             if q in spans[up]:
-                source = source - dot3(solved[up], upper_block(q, trailing(up)), False)
-        solved[q] = dot3(source, upper_block(q, 0), False)
+                solved[q] = solved[q] - dot3(solved[up], upper_block(q, trailing(up)), False)
         xs[q] = solved[q]
     for level in range(4):
         q = (g // (1 << level)) * (1 << level) + (1 << level) - 1
         xpath[level] = xs[q] * exists(g, level).astype(f32)
 
     across = jnp.concatenate([xpath[0], xpath[1], xpath[2], xpath[3]], axis=1)
-    x1 = dot3(ftop[1] - dot3(across, top_stack(1), False), top_block(1, 0), False)
-    x2 = dot3(ftop[2] - dot3(across, top_stack(2), False), top_block(2, 0), False)
-    x0 = dot3(
-        ftop[0] - dot3(across, top_stack(0), False) - dot3(x1, top_block(0, 1), False), top_block(0, 0), False
-    )
+    x1 = ftop[1] - dot3(across, top_stack(1), False)
+    x2 = ftop[2] - dot3(across, top_stack(2), False)
+    x0 = ftop[0] - dot3(across, top_stack(0), False) - dot3(x1, top_block(0, 1), False)
     zown[0], zown[1], zown[6] = x0, x1, x2
     zown[2:6] = xpath[...]
 
@@ -481,37 +492,35 @@
     for i in range(1, 4):
         z_from(i).wait_recv()
 
-    def back_piece(j):
-        at = pl.ds(leaf - (j + 1) * CHUNK, CHUNK)
-        return remote(zbuf.at[at], o_leaf.at[at], s_back, r_back, (other, zo))
-
-    def keep_piece(j):
-        at = pl.ds(leaf - (j + 1) * CHUNK, CHUNK)
-        return pltpu.make_async_copy(zbuf.at[at], o_leaf.at[at], l_sem.at[0])
-
-    def let_go(j):
+    def back_piece(s):
+        return remote(zbuf.at[s], o_leaf.at[s], s_back, r_back, (other, zo))
+
+    def keep_piece(s):
+        return pltpu.make_async_copy(zbuf.at[s], o_leaf.at[s], l_sem.at[0])
+
+    def let_go(s):
         @pl.when(hub)
         def _():
-            keep_piece(j).start()
+            keep_piece(s).start()
 
         @pl.when(guest)
         def _():
-            back_piece(j).start()
+            back_piece(s).start()
+
+    def backward_step(s):
+        b, d = leaf_block(s)
+        z_at = jnp.concatenate([zbuf[s + 1], zbuf[slot_of(s, 1)], zbuf[slot_of(s, 2)]], axis=1)
+        zbuf[s] = dot3(fwd[s] - dot3(z_at, b, False), d, False)
+
+    backward_step(leaf - 1)
 
     def backward(j, carry):
-        for i in range(CHUNK):
-            s = leaf - 1 - j * CHUNK - i
-            b, d = leaf_block(s)
-            z_at = jnp.concatenate([zbuf[s + 1], zbuf[slot_of(s, 1)], zbuf[slot_of(s, 2)]], axis=1)
-            zbuf[s] = dot3(fwd[s] - dot3(z_at, b, False), d, False)
-
-        @pl.when(j >= 1)
-        def _():
-            let_go(j - 1)
-
+        s = leaf - 2 - j
+        backward_step(s)
+        let_go(s + 1)
         return carry
 
-    lax.fori_loop(0, chunks, backward, 0)
+    lax.fori_loop(0, leaf - 1, backward, 0)
 
     for k in range(4):
 
@@ -521,7 +530,7 @@
 
     top_out = pltpu.make_async_copy(tout, o_top.at[0], l_sem.at[1])
     top_out.start()
-    let_go(chunks - 1)
+    let_go(0)
 
     whole = pl.ds(0, leaf)
 
@@ -532,7 +541,8 @@
 
     left(s_own.at[0], z)
     for i in range(3):
-        top_z_all(i).wait_send()
+        if i < 2:
+            top_z_all(i).wait_send()
         share_group(i).wait_send()
         share_part(i + 1).wait_send()
         share_z(i + 1).wait_send()

time: 102 us -> 97.1 us (0.952)
  Pallas kernels: 99.8 us -> 94.8 us
    pallas_call x1, Pallas kernels: 99.8 us -> 94.8 us  [local(): pl.pallas_call(kernel, out_shape=(jax.ShapeDtypeStruct(rl.shape, f32), ja...]
where the time goes in v5:
time: 97.1 us; the launch traced here: 97 us
  Pallas kernels  94.8 us (98%)
  local copies, waits for them, and re-layouts  1.59 us (2%)
    pallas_call x1, Pallas kernels, local(): pl.pallas_call(kernel, out_shape=(jax.ShapeDtypeStruct(rl.shape, f32), ja...  94.8 us

profile of v5, /device:TPU:1, one launch (start us, length us, event | category | flops | bytes accessed | tf_op | source)
XLA Modules:
  0.0 97.0 jit_solution(9254769935123843584)
XLA Ops:
  0.6 94.8 %substitution.1 = (f32[32,64,128]{2,1,0:T(8,128)S(1)}, f32[1,64,128]{2,1,0:T(8,128)S(1)}) custom-call(s32[3,32]{1,0:T(4,128)} %bitcast.1, f32[32,64,128]{2,1,0:T(8,128)} %rl.1, f32[1,64,128]{2,1,0:T(8,128)} %rt.1, f32[32,3,32,128]{3,2,1,0:T(8,128)} %lb.1, f32[32,32,128]{2,1,0:T(8,128)} %ld.1, f32[32,1,32,128]{3,2,1,0:T(8,128)} %tb.1, f32[1,32,128]{2,1,0:T(8,128)} %td.1), custom_call_target="tpu_custom_call" | custom-call | tf_op jit(solution)/shard_map/substitution/pallas_call | solution.py:599
  95.4 1.0 %copy.11 = f32[32,64,128]{2,1,0:T(8,128)} copy(f32[32,64,128]{2,1,0:T(8,128)S(1)} %get-tuple-element.4) | data formatting | bytes 2097152
  96.4 0.6 copy.12

commit v6 on v5

--- a/solution.py
+++ b/solution.py
@@ -74,7 +74,8 @@
         return 4 * lax.rem(g + i, 8) + c
 
     def mate(k, i):
-        to = lax.rem(k + i, 4)
+        dy, dr = ((1, 1), (1, 0), (0, 1))[i - 1]
+        to = 2 * ((c // 2 + dy) % 2) + (role + dr) % 2
         return to, (4 * g + 2 * (to // 2) + core, jnp.where(to % 2 == role, z, zo))
 
     def worker(k):
@@ -269,7 +270,14 @@
             m2 = (second == t).astype(f32)
             acc[t] = acc[t] - (m1 * out1 + m2 * out2)
 
-        for t in range(2, leaf + 6):
+        for start in range(0, leaf, 8):
+
+            @pl.when(s + 2 < min(start + 8, leaf))
+            def _(start=start):
+                for t in range(max(start, 2), min(start + 8, leaf)):
+                    push(t)
+
+        for t in range(leaf, leaf + 6):
             push(t)
 
     def turn(j, carry):
@@ -461,7 +469,7 @@
         return remote(zown.at[pl.ds(0, 6)], zbuf.at[pl.ds(leaf, 6), my_cols], s_z.at[i], r_z.at[i], device)
 
     def z_from(i):
-        view = zbuf.at[pl.ds(leaf, 6), at_cols(lax.rem(place + 4 - i, 4))]
+        view = zbuf.at[pl.ds(leaf, 6), at_cols(mate(place, i)[0])]
         return remote(zown.at[pl.ds(0, 6)], view, s_z.at[i], r_z.at[i], mate(place, i)[1])
 
     for i in range(1, 4):

time: 97.1 us -> 96.3 us (level)
  no operation moved by 1% of the time
where the time goes in v6:
time: 96.3 us; the launch traced here: 96.2 us
  Pallas kernels  93.9 us (98%)
  local copies, waits for them, and re-layouts  1.59 us (2%)
    pallas_call x1, Pallas kernels, local(): pl.pallas_call(kernel, out_shape=(jax.ShapeDtypeStruct(rl.shape, f32), ja...  93.9 us

profile of v6, /device:TPU:1, one launch (start us, length us, event | category | flops | bytes accessed | tf_op | source)
XLA Modules:
  0.0 96.2 jit_solution(4262139210284714724)
XLA Ops:
  0.6 93.9 %substitution.1 = (f32[32,64,128]{2,1,0:T(8,128)S(1)}, f32[1,64,128]{2,1,0:T(8,128)S(1)}) custom-call(s32[3,32]{1,0:T(4,128)} %bitcast.1, f32[32,64,128]{2,1,0:T(8,128)} %rl.1, f32[1,64,128]{2,1,0:T(8,128)} %rt.1, f32[32,3,32,128]{3,2,1,0:T(8,128)} %lb.1, f32[32,32,128]{2,1,0:T(8,128)} %ld.1, f32[32,1,32,128]{3,2,1,0:T(8,128)} %tb.1, f32[1,32,128]{2,1,0:T(8,128)} %td.1), custom_call_target="tpu_custom_call" | custom-call | tf_op jit(solution)/shard_map/substitution/pallas_call | solution.py:607
  94.6 1.0 %copy.11 = f32[32,64,128]{2,1,0:T(8,128)} copy(f32[32,64,128]{2,1,0:T(8,128)S(1)} %get-tuple-element.4) | data formatting | bytes 2097152
  95.6 0.6 copy.12

commit v7 on v6

--- a/solution.py
+++ b/solution.py
@@ -160,9 +160,9 @@
 
         @pl.when(guest)
         def _():
-            rhs_piece(j).start()
             for copy in own(j, 0, 1, (sn, zo)):
                 copy.start()
+            rhs_piece(j).start()
 
     send_own(0)
 
@@ -403,11 +403,11 @@
         view = gathered.at[at, level]
         return remote(view, view, s_con.at[0, level], r_con.at[at, level], (4 * at + c, z))
 
-    for level in range(4):
-
-        @pl.when(exists(g, level))
-        def _(level=level):
-            for i in (4, 3, 5, 2, 6, 1, 7):
+    for i in (5, 3, 4, 2, 6, 1, 7):
+        for level in range(4):
+
+            @pl.when(exists(g, level))
+            def _(i=i, level=level):
                 share_contrib(i, level).start()
 
     gathered[g] = contrib[...]

time: 96.3 us -> 96.2 us (level)
  no operation moved by 1% of the time
where the time goes in v7:
time: 96.2 us; the launch traced here: 96.1 us
  Pallas kernels  93.9 us (98%)
  local copies, waits for them, and re-layouts  1.59 us (2%)
    pallas_call x1, Pallas kernels, local(): pl.pallas_call(kernel, out_shape=(jax.ShapeDtypeStruct(rl.shape, f32), ja...  93.9 us

profile of v7, /device:TPU:1, one launch (start us, length us, event | category | flops | bytes accessed | tf_op | source)
XLA Modules:
  0.0 96.1 jit_solution(4269248535001595436)
XLA Ops:
  0.6 93.9 %substitution.1 = (f32[32,64,128]{2,1,0:T(8,128)S(1)}, f32[1,64,128]{2,1,0:T(8,128)S(1)}) custom-call(s32[3,32]{1,0:T(4,128)} %bitcast.1, f32[32,64,128]{2,1,0:T(8,128)} %rl.1, f32[1,64,128]{2,1,0:T(8,128)} %rt.1, f32[32,3,32,128]{3,2,1,0:T(8,128)} %lb.1, f32[32,32,128]{2,1,0:T(8,128)} %ld.1, f32[32,1,32,128]{3,2,1,0:T(8,128)} %tb.1, f32[1,32,128]{2,1,0:T(8,128)} %td.1), custom_call_target="tpu_custom_call" | custom-call | tf_op jit(solution)/shard_map/substitution/pallas_call | solution.py:607
  94.5 1.0 %copy.11 = f32[32,64,128]{2,1,0:T(8,128)} copy(f32[32,64,128]{2,1,0:T(8,128)S(1)} %get-tuple-element.4) | data formatting | bytes 2097152
  95.5 0.6 copy.12
